TPU v7x, 128 devices: a whole 4x4x4 slice. The times are simulated.
128 devices in a mesh: rows: 16 (over x_hi, y, core), seq: 8 (over x_lo, z).
Axes of the slice: x: 4 (x_hi: 2, x_lo: 2; x = x_hi * 2 + x_lo), y: 4, z: 4, core: 2. Of those that a mesh axis runs over, the one named last changes fastest.
Arguments:
- block_input: bfloat16 [64, 1024, 1024], P('rows', 'seq'), may hold values from -6 to 6
- segment_ids: int32 [64, 1024], P('rows'), may hold values from 0 to 3, never falling along the last dimension, each value on 1 to 512 neighbouring positions
- padding_flags: int32 [64, 1024], P('rows'), may hold values 0 or 1
- cotangent: bfloat16 [64, 1024, 1024], P('rows', 'seq'), may hold values from -6 to 6
- norm_one_gain: bfloat16 [1024], replicated, may hold values from 0.5 to 1.5
- norm_one_bias: bfloat16 [1024], replicated, may hold values from -1.75 to 1.75
- query_key_value: bfloat16 [1024, 3072], replicated, may hold values from -0.1875 to 0.1875
- query_value_bias: bfloat16 [2048], replicated, may hold values from -1.75 to 1.75
- out_weight: bfloat16 [1024, 1024], replicated, may hold values from -0.75 to 0.75
- out_bias: bfloat16 [1024], replicated, may hold values from -1.75 to 1.75
- norm_two_gain: bfloat16 [1024], replicated, may hold values from 0.5 to 1.5
- norm_two_bias: bfloat16 [1024], replicated, may hold values from -1.75 to 1.75
- up_weight: bfloat16 [1024, 4096], replicated, may hold values from -0.1875 to 0.1875
- up_bias: bfloat16 [4096], replicated, may hold values from -1.75 to 1.75
- down_weight: bfloat16 [4096, 1024], replicated, may hold values from -0.09375 to 0.09375
- down_bias: bfloat16 [1024], replicated, may hold values from -1.75 to 1.75
Outputs:
- layer_out: bfloat16 [64, 1024, 1024], P('rows', 'seq')
- grad_input: bfloat16 [64, 1024, 1024], P('rows', 'seq')
- grad_norm_one_gain: float32 [1024], P(('rows', 'seq'))
- grad_norm_one_bias: float32 [1024], P(('rows', 'seq'))
- grad_query_key_value: float32 [1024, 3072], P(('rows', 'seq'))
- grad_query_value_bias: float32 [2048], P(('rows', 'seq'))
- grad_out_weight: float32 [1024, 1024], P(('rows', 'seq'))
- grad_out_bias: float32 [1024], P(('rows', 'seq'))
- grad_norm_two_gain: float32 [1024], P(('rows', 'seq'))
- grad_norm_two_bias: float32 [1024], P(('rows', 'seq'))
- grad_up_weight: float32 [1024, 4096], P(('rows', 'seq'))
- grad_up_bias: float32 [4096], P(('rows', 'seq'))
- grad_down_weight: float32 [4096, 1024], P(('rows', 'seq'))
- grad_down_bias: float32 [1024], P(('rows', 'seq'))
Inputs may be any that keep to these rules, and one draw needn't show every extreme that they name: `segment_ids`: along each row the ids never fall; each document holds 1 to 512 positions, and some document holds exactly that many.
All inputs are finite; a program needn't handle non-finite values. No bound on the sum of `padding_flags` on one device may be relied on, other than what follows from the above.
Results may differ from a plain program's by a relative error of at most 0.017.
Values may be sent and summed in bfloat16 or wider, within the bound.
A program may use at most 256 MiB of HBM per device.

v0:
```python
from functools import partial

import jax
import jax.numpy as jnp
from jax import lax
from jax.sharding import PartitionSpec as P

HEAD_DIM = 64


def layer_norm(values, gain, shift):
    center = values - jnp.mean(values, axis=-1, keepdims=True)
    variance = jnp.mean(center * center, axis=-1, keepdims=True)
    return center * lax.rsqrt(variance + 1e-05) * gain + shift


def allowed_keys(segment_row, flag_row):
    count = segment_row.shape[0]
    position = lax.broadcasted_iota(jnp.int32, (count, count), 0)
    column = lax.broadcasted_iota(jnp.int32, (count, count), 1)
    same = segment_row[:, None] == segment_row[None, :]
    return same & (column <= position) & ((flag_row[None, :] == 0) | (column == position))


def split_heads(packed):
    full_len = packed.shape[0]
    local_heads = packed.shape[2] // HEAD_DIM
    query = packed[:, 0].reshape(full_len, local_heads, HEAD_DIM)
    keys_row = packed[:, 1].reshape(full_len, local_heads, HEAD_DIM)
    value_row = packed[:, 2].reshape(full_len, local_heads, HEAD_DIM)
    return (query, keys_row, value_row)


def masked_scores(query, keys_row, segment_row, flag_row):
    scores = jnp.einsum(
        "qhd,khd->hqk", query, keys_row, preferred_element_type=jnp.float32
    ) * HEAD_DIM ** (-0.5)
    return jnp.where(allowed_keys(segment_row, flag_row)[None], scores, -1e30)


def attend_forward(items):
    packed, segment_row, flag_row = items
    query, keys_row, value_row = split_heads(packed)
    scores = masked_scores(query, keys_row, segment_row, flag_row)
    row_max = jnp.max(scores, axis=-1, keepdims=True)
    expo = jnp.exp(scores - row_max)
    totals = jnp.sum(expo, axis=-1, keepdims=True)
    prob_low = (expo / totals).astype(jnp.bfloat16)
    log_total = (row_max + jnp.log(totals))[..., 0]
    context = jnp.einsum("hqk,khd->qhd", prob_low, value_row, preferred_element_type=jnp.float32)
    return (context.astype(jnp.bfloat16).reshape(packed.shape[0], packed.shape[2]), log_total)


def attend_backward(items):
    packed, grad_row, log_total, segment_row, flag_row = items
    full_len = packed.shape[0]
    query, keys_row, value_row = split_heads(packed)
    scores = masked_scores(query, keys_row, segment_row, flag_row)
    probs = jnp.exp(scores - log_total[..., None])
    prob_low = probs.astype(jnp.bfloat16)
    grad_ctx = grad_row.reshape(full_len, query.shape[1], HEAD_DIM)
    grad_probs = jnp.einsum("qhd,khd->hqk", grad_ctx, value_row, preferred_element_type=jnp.float32)
    inner = jnp.sum(probs * grad_probs, axis=-1, keepdims=True)
    grad_scores = (probs * (grad_probs - inner)).astype(jnp.bfloat16)
    scale = HEAD_DIM ** (-0.5)
    grad_query = (
        jnp.einsum("hqk,khd->qhd", grad_scores, keys_row, preferred_element_type=jnp.float32)
        * scale
    )
    grad_keys = (
        jnp.einsum("hqk,qhd->khd", grad_scores, query, preferred_element_type=jnp.float32) * scale
    )
    grad_value = jnp.einsum("hqk,qhd->khd", prob_low, grad_ctx, preferred_element_type=jnp.float32)
    stacked = jnp.stack([grad_query, grad_keys, grad_value], axis=1)
    return stacked.reshape(full_len, 3, packed.shape[2]).astype(jnp.bfloat16)


def contract_rows(left, right):
    return lax.dot_general(
        left, right, (((0,), (0,)), ((), ())), preferred_element_type=jnp.float32
    )


def contract_cols(left, right):
    return lax.dot_general(
        left, right, (((1,), (1,)), ((), ())), preferred_element_type=jnp.float32
    )


def on_device(
    block_input,
    segment_ids,
    padding_flags,
    cotangent,
    norm_one_gain,
    norm_one_bias,
    query_key_value,
    query_value_bias,
    out_weight,
    out_bias,
    norm_two_gain,
    norm_two_bias,
    up_weight,
    up_bias,
    down_weight,
    down_bias,
):
    row_count, local_len, feature_width = block_input.shape
    token_count = row_count * local_len
    flat_in = block_input.astype(jnp.float32).reshape(token_count, feature_width)
    normed_one, norm_one_back = jax.vjp(
        layer_norm, flat_in, norm_one_gain.astype(jnp.float32), norm_one_bias.astype(jnp.float32)
    )
    normed_low = normed_one.astype(jnp.bfloat16)
    qv_bias = query_value_bias.astype(jnp.float32)
    bias_full = jnp.concatenate(
        [qv_bias[:feature_width], jnp.zeros((feature_width,), jnp.float32), qv_bias[feature_width:]]
    )
    qkv_local = jnp.dot(normed_low, query_key_value, preferred_element_type=jnp.float32) + bias_full
    qkv_local = qkv_local.astype(jnp.bfloat16).reshape(row_count, local_len, 3, feature_width)
    qkv_heads = lax.all_to_all(qkv_local, "seq", split_axis=3, concat_axis=1, tiled=True)
    ctx_heads, log_totals = lax.map(attend_forward, (qkv_heads, segment_ids, padding_flags))
    context = lax.all_to_all(ctx_heads, "seq", split_axis=1, concat_axis=2, tiled=True).reshape(
        token_count, feature_width
    )
    attn = jnp.dot(context, out_weight, preferred_element_type=jnp.float32) + out_bias.astype(
        jnp.float32
    )
    resid = flat_in + attn
    normed_two, norm_two_back = jax.vjp(
        layer_norm, resid, norm_two_gain.astype(jnp.float32), norm_two_bias.astype(jnp.float32)
    )
    second_low = normed_two.astype(jnp.bfloat16)
    up_val = jnp.dot(second_low, up_weight, preferred_element_type=jnp.float32) + up_bias.astype(
        jnp.float32
    )
    act, gelu_back = jax.vjp(partial(jax.nn.gelu, approximate=True), up_val)
    act_low = act.astype(jnp.bfloat16)
    down_val = jnp.dot(act_low, down_weight, preferred_element_type=jnp.float32) + down_bias.astype(
        jnp.float32
    )
    layer_out = (resid + down_val).astype(jnp.bfloat16).reshape(row_count, local_len, feature_width)
    grad_out = cotangent.reshape(token_count, feature_width)
    grad_out_f = grad_out.astype(jnp.float32)
    grad_down_weight = contract_rows(act_low, grad_out)
    grad_down_bias = jnp.sum(grad_out_f, axis=0)
    grad_act = contract_cols(grad_out, down_weight)
    grad_up_val = gelu_back(grad_act)[0].astype(jnp.bfloat16)
    grad_up_bias = jnp.sum(grad_up_val.astype(jnp.float32), axis=0)
    grad_up_weight = contract_rows(second_low, grad_up_val)
    grad_normed_two = contract_cols(grad_up_val, up_weight)
    grad_resid_norm, grad_norm_two_gain, grad_norm_two_bias = norm_two_back(grad_normed_two)
    grad_resid = grad_out_f + grad_resid_norm
    grad_attn = grad_resid.astype(jnp.bfloat16)
    grad_out_bias = jnp.sum(grad_attn.astype(jnp.float32), axis=0)
    grad_out_weight = contract_rows(context, grad_attn)
    grad_context = contract_cols(grad_attn, out_weight).astype(jnp.bfloat16)
    grad_context = grad_context.reshape(row_count, local_len, feature_width)
    grad_ctx_heads = lax.all_to_all(grad_context, "seq", split_axis=2, concat_axis=1, tiled=True)
    grad_qkv_heads = lax.map(
        attend_backward, (qkv_heads, grad_ctx_heads, log_totals, segment_ids, padding_flags)
    )
    grad_qkv = lax.all_to_all(grad_qkv_heads, "seq", split_axis=1, concat_axis=3, tiled=True)
    grad_qkv = grad_qkv.reshape(token_count, 3 * feature_width)
    grad_qkv_f = grad_qkv.astype(jnp.float32)
    grad_query_value_bias = jnp.concatenate(
        [
            jnp.sum(grad_qkv_f[:, :feature_width], axis=0),
            jnp.sum(grad_qkv_f[:, 2 * feature_width :], axis=0),
        ]
    )
    grad_query_key_value = contract_rows(normed_low, grad_qkv)
    grad_normed_one = contract_cols(grad_qkv, query_key_value)
    grad_input_norm, grad_norm_one_gain, grad_norm_one_bias = norm_one_back(grad_normed_one)
    grad_input = (
        (grad_resid + grad_input_norm)
        .astype(jnp.bfloat16)
        .reshape(row_count, local_len, feature_width)
    )
    partials = (
        grad_norm_one_gain,
        grad_norm_one_bias,
        grad_query_key_value,
        grad_query_value_bias,
        grad_out_weight,
        grad_out_bias,
        grad_norm_two_gain,
        grad_norm_two_bias,
        grad_up_weight,
        grad_up_bias,
        grad_down_weight,
        grad_down_bias,
    )
    summed = (
        lax.psum_scatter(partials[0], ("rows", "seq"), scatter_dimension=0, tiled=True),
        lax.psum_scatter(partials[1], ("rows", "seq"), scatter_dimension=0, tiled=True),
        lax.psum_scatter(partials[2], ("rows", "seq"), scatter_dimension=0, tiled=True),
        lax.psum_scatter(partials[3], ("rows", "seq"), scatter_dimension=0, tiled=True),
        lax.psum_scatter(partials[4], ("rows", "seq"), scatter_dimension=0, tiled=True),
        lax.psum_scatter(partials[5], ("rows", "seq"), scatter_dimension=0, tiled=True),
        lax.psum_scatter(partials[6], ("rows", "seq"), scatter_dimension=0, tiled=True),
        lax.psum_scatter(partials[7], ("rows", "seq"), scatter_dimension=0, tiled=True),
        lax.psum_scatter(partials[8], ("rows", "seq"), scatter_dimension=0, tiled=True),
        lax.psum_scatter(partials[9], ("rows", "seq"), scatter_dimension=0, tiled=True),
        lax.psum_scatter(partials[10], ("rows", "seq"), scatter_dimension=0, tiled=True),
        lax.psum_scatter(partials[11], ("rows", "seq"), scatter_dimension=0, tiled=True),
    )
    return (
        layer_out,
        grad_input,
        summed[0],
        summed[1],
        summed[2],
        summed[3],
        summed[4],
        summed[5],
        summed[6],
        summed[7],
        summed[8],
        summed[9],
        summed[10],
        summed[11],
    )


def solution(mesh):
    return jax.shard_map(
        on_device,
        mesh=mesh,
        in_specs=(
            P("rows", "seq", None),
            P("rows", None),
            P("rows", None),
            P("rows", "seq", None),
            P(),
            P(),
            P(),
            P(),
            P(),
            P(),
            P(),
            P(),
            P(),
            P(),
            P(),
            P(),
        ),
        out_specs=(
            P("rows", "seq", None),
            P("rows", "seq", None),
            P(("rows", "seq")),
            P(("rows", "seq")),
            P(("rows", "seq"), None),
            P(("rows", "seq")),
            P(("rows", "seq"), None),
            P(("rows", "seq")),
            P(("rows", "seq")),
            P(("rows", "seq")),
            P(("rows", "seq"), None),
            P(("rows", "seq")),
            P(("rows", "seq"), None),
            P(("rows", "seq")),
        ),
        check_vma=False,
    )
```

profile of v0, /device:TPU:1, one launch (start us, length us, event | category | flops | bytes accessed | tf_op | source)
XLA Modules:
  0.0 2853.3 jit_solution(6446587881926820113)
XLA Ops:
  14.3 7.6 add_convert_fusion
  21.9 10.1 reshape.375
  32.0 7.4 copy.78
  39.4 6.8 all-to-all-start
  46.2 37.5 %all-to-all-done = bf16[4,128,3,1024]{1,0,2,3:T(4,128)(2,1)} async-done(((bf16[4,128,3,1024]{1,0,2,3:T(4,128)(2,1)}), bf16[4,128,3,1024]{1,0,2,3:T(4,128)(2,1)}, u32[]{:S(2)}, u32[]{:S(2)}) %all-to-all-start) | async-done | bytes 3145760 | tf_op jit(solution)/shard_map/all_to_all | solution.py:121
  83.6 4.1 copy.79
  87.8 4.7 copy.80
  92.5 4.7 copy.81
  97.2 42.5 %while.22 = (s32[]{:T(128)}, bf16[4,1024,128]{1,2,0:T(8,128)(2,1)}, f32[4,2,1024]{2,1,0:T(2,128)S(1)}, bf16[4,1024,3,128]{1,3,2,0:T(8,128)(2,1)}, s32[4,1024]{1,...) while((s32[]{:T(128)}, bf16[4,1024,128]{1,2,0:T(8,128)(2,1)}, f32[4,2,1024]{2,1,0:T(2,128)S(1)}, ...), condition=%wide.region_5.6_spmd, body=%wide.region_2.5_spmd.sunk | while | flops 568458240 | bytes 34163292 | solution.py:122
  97.2 1.8 fusion.126
  100.3 1.9 fusion.127
  102.2 2.0 fusion.128
  104.3 2.8 fusion.129
  111.0 1.9 fusion.127
  112.9 2.0 fusion.128
  114.9 2.8 fusion.129
  118.5 1.8 fusion.126
  121.6 1.9 fusion.127
  123.5 2.0 fusion.128
  125.5 2.8 fusion.129
  132.2 1.9 fusion.127
  134.2 2.0 fusion.128
  136.2 2.8 fusion.129
  139.7 2.5 copy.82
  142.2 4.5 all-to-all-start.1
  146.8 14.9 all-to-all-done.1
  161.7 1.9 copy.83
  165.4 10.8 fusion.56
  176.2 14.2 convert_reduce_fusion
  190.4 5.5 multiply_reduce_fusion.1
  197.9 2.3 convolution_convert_fusion
  200.2 2.5 copy.84
  202.7 3.6 all-to-all-start.2
  206.4 3.3 fusion.46
  209.7 11.6 all-to-all-done.2
  222.6 65.6 %while.23 = (s32[]{:T(128)}, bf16[4,1024,3,128]{1,3,2,0:T(8,128)(2,1)}, bf16[4,1024,3,128]{1,3,2,0:T(8,128)(2,1)}, s32[4,1024]{1,0:T(4,128)S(1)}, s32[4,1024]{1,...) while((s32[]{:T(128)}, ...), condition=%wide.region_12.13_spmd, body=%wide.region_10.12_spmd.sunk | while | flops 1382939648 | bytes 75049576 | solution.py:160
  227.2 3.4 multiply_reduce_fusion.5
  230.6 2.7 multiply_convert_fusion.5
  235.6 2.5 fusion.143
  243.5 3.4 multiply_reduce_fusion.5
  247.0 2.7 multiply_convert_fusion.5
  251.9 2.5 fusion.143
  259.9 3.4 multiply_reduce_fusion.5
  263.4 2.7 multiply_convert_fusion.5
  268.3 2.5 fusion.143
  276.3 3.4 multiply_reduce_fusion.5
  279.7 2.7 multiply_convert_fusion.5
  284.7 2.5 fusion.143
  288.2 6.0 copy.87
  294.2 4.6 all-to-all-start.3
  299.4 38.1 %all-to-all-done.3 = bf16[4,1024,3,128]{3,0,2,1:T(4,128)(2,1)} async-done(((bf16[4,1024,3,128]{3,0,2,1:T(4,128)(2,1)}), bf16[4,1024,3,128]{3,0,2,1:T(4,128)(2,1)}, u32[]{:S(2)}, u32[]{:S(2)}) %all-to-all-start.3) | async-done | bytes 3145760 | tf_op jit(solution)/shard_map/all_to_all | solution.py:163
  337.6 5.6 copy.107
  343.1 6.0 reshape.373
  349.2 8.2 fusion.67
  359.0 10.5 fusion.55
  370.7 15.4 fusion.57
  387.0 13.0 add_convert_fusion.2
  401.5 6.1 fusion.58
  410.0 67.3 %all-reduce.8 = (f32[1024]{0:T(1024)S(1)}, f32[1024]{0:T(1024)S(1)}, f32[2048]{0:T(1024)S(1)}, f32[1024]{0:T(1024)S(1)}, f32[1024]{0:T(1024)S(1)}, /*index=5*/f3...) all-reduce(f32[1024]{0:T(1024)S(1)} %get-tuple-element.130, ...), channel_id=2, replica_groups=mesh['rows'=16,'seq'=8] {'rows','seq'}, use_global_device_ids=true, to_apply=%region_16.17.clone | all-reduce | flops 12288 | bytes 98304
  482.0 3.8 add_convert_fusion.1
  485.8 368.9 %reduce-scatter.7.cloned.1.call-done = f32[8,1024]{1,0:T(8,128)} async-done(((f32[1024,1024]{1,0:T(8,128)}), f32[8,1024]{1,0:T(8,128)}) %reduce-scatter.7.cloned.1.call-update) | async-done | bytes 32784 | tf_op jit(solution)/shard_map/reduce_scatter | solution.py:199
  854.7 658.1 %reduce-scatter.5.cloned.1.call-done = f32[8,3072]{1,0:T(8,128)} async-done(((f32[1024,3072]{1,0:T(8,128)}), f32[8,3072]{1,0:T(8,128)}) %reduce-scatter.5.cloned.1.call-update) | async-done | bytes 98320 | tf_op jit(solution)/shard_map/reduce_scatter | solution.py:197
  1512.9 666.5 %reduce-scatter.9.cloned.1.call-done = f32[8,4096]{1,0:T(8,128)} async-done(((f32[1024,4096]{1,0:T(8,128)}), f32[8,4096]{1,0:T(8,128)}) %reduce-scatter.9.cloned.1.call-update) | async-done | bytes 131088 | tf_op jit(solution)/shard_map/reduce_scatter | solution.py:203
  2179.3 666.9 %reduce-scatter.11.cloned.1.call-done = f32[32,1024]{1,0:T(8,128)} async-done(((f32[4096,1024]{1,0:T(8,128)}), f32[32,1024]{1,0:T(8,128)}) %reduce-scatter.11.cloned.1.call-update) | async-done | bytes 131088 | tf_op jit(solution)/shard_map/reduce_scatter | solution.py:205
  (218 shorter events, 67.4 us)
Async XLA Ops:
  7.2 156.4 %copy-start = (bf16[1024,1024]{1,0:T(8,128)(2,1)S(1)}, bf16[1024,1024]{1,0:T(8,128)(2,1)}, u32[]{:S(2)}) copy-start(bf16[1024,1024]{1,0:T(8,128)(2,1)} %param.28) | copy-start | bytes 6291460
  8.8 3.8 copy-start.29
  8.8 3.8 copy-start.23
  10.4 2.1 copy-start.21
  10.5 2.1 copy-start.25
  11.2 1.4 copy-start.15
  11.8 0.8 copy-start.19
  39.4 44.3 %all-to-all-start = ((bf16[4,128,3,1024]{1,0,2,3:T(4,128)(2,1)}), bf16[4,128,3,1024]{1,0,2,3:T(4,128)(2,1)}, u32[]{:S(2)}, u32[]{:S(2)}) async-start(bf16[4,128,3,1024]{1,0,2,3:T(4,128)(2,1)} %copy.78), calls=%async_computation | async-start | bytes 6291456 | tf_op jit(solution)/shard_map/all_to_all | solution.py:121
  92.5 4.7 copy-start.17
  92.5 4.7 copy-start.18
  139.7 7.0 copy-start.40
  139.7 7.0 copy-start.41
  139.7 7.0 copy-start.42
  139.7 7.0 copy-start.35
  139.7 23.9 copy-start.2
  142.2 19.4 all-to-all-start.1
  146.8 18.6 copy-start.38
  146.8 29.4 %copy-start.33 = (f32[4096]{0:T(1024)}, f32[4096]{0:T(1024)S(1)}, u32[]{:S(2)}) copy-start(f32[4096]{0:T(1024)S(1)} %convert_element_type.107) | copy-start | bytes 49156
  163.6 1.4 copy-start.13
  165.0 31.0 %copy-start.9 = (f32[512,1024]{1,0:T(8,128)}, f32[512,1024]{1,0:T(8,128)S(1)}, u32[]{:S(2)}) copy-start(f32[512,1024]{1,0:T(8,128)S(1)} %get-tuple-element.190) | copy-start | bytes 6291460
  165.4 10.8 copy-start.6
  165.4 25.0 slice-start
  176.2 14.2 slice-start.1
  190.4 5.5 copy-start.44
  196.6 3.5 copy-start.4
  196.7 3.5 copy-start.27
  197.9 2.3 copy-start.11
  200.2 6.2 copy-start.14
  200.2 6.2 copy-start.12
  202.7 18.5 all-to-all-start.2
  206.4 648.4 %reduce-scatter.7.cloned.1.call-start = ((), (), s32[]{:S(2)}) async-start(), calls=%async_computation.9 | async-start | bytes 4227072 | tf_op jit(solution)/shard_map/reduce_scatter | solution.py:199
  294.2 4.7 copy-start.22
  294.2 4.7 copy-start.3
  294.2 4.7 copy-start.16
  294.2 4.7 copy-start.20
  294.2 4.7 copy-start.30
  294.2 43.3 %all-to-all-start.3 = ((bf16[4,1024,3,128]{3,0,2,1:T(4,128)(2,1)}), bf16[4,1024,3,128]{3,0,2,1:T(4,128)(2,1)}, u32[]{:S(2)}, u32[]{:S(2)}) async-start(bf16[4,1024,3,128]{3,0,2,1:T(4,128)(2,1)} %copy.87), calls=%async_computation.3 | async-start | bytes 6291456 | tf_op jit(solution)/shard_map/all_to_all | solution.py:163
  298.8 1214.0 %reduce-scatter.5.cloned.1.call-start = ((), (), s32[]{:S(2)}) async-start(), calls=%async_computation.8 | async-start | bytes 12681216 | tf_op jit(solution)/shard_map/reduce_scatter | solution.py:197
  357.4 1.6 copy-start.10
  357.4 1.6 copy-start.39
  357.4 1821.9 %reduce-scatter.9.cloned.1.call-start = ((), (), s32[]{:S(2)}) async-start(), calls=%async_computation.10 | async-start | bytes 16908288 | tf_op jit(solution)/shard_map/reduce_scatter | solution.py:203
  369.4 1.2 copy-start.7
  369.4 1.2 copy-start.34
  369.5 2476.8 %reduce-scatter.11.cloned.1.call-start = ((), (), s32[]{:S(2)}) async-start(), calls=%async_computation.11 | async-start | bytes 16908288 | tf_op jit(solution)/shard_map/reduce_scatter | solution.py:205
  386.1 0.7 copy-start.43
  387.0 13.0 copy-start.5
  400.8 0.7 copy-start.24
  401.5 7.5 copy-start.26
  401.5 8.5 copy-start.31
  401.5 8.5 copy-start.32
  401.5 8.5 copy-start.36
  401.5 8.5 copy-start.37
  401.5 80.5 %copy-start.28 = (f32[512]{0:T(512)S(1)}, f32[512]{0:T(512)}, u32[]{:S(2)}) copy-start(f32[512]{0:T(512)} %copy-done.27) | copy-start | bytes 6148
  407.6 1.3 copy-start.8
  408.9 2437.4 %copy-start.1 = (bf16[1024,1024]{1,0:T(8,128)(2,1)S(1)}, bf16[1024,1024]{1,0:T(8,128)(2,1)}, u32[]{:S(2)}) copy-start(bf16[1024,1024]{1,0:T(8,128)(2,1)} %param.28) | copy-start | bytes 6291460
Sparse Core Ops, SparseCore 0:
  210.1 644.5 reduce-scatter.6
  857.8 654.9 reduce-scatter.4
  1515.8 663.4 reduce-scatter.8
  2182.2 664.0 reduce-scatter.10
where the time goes:
time: 2880 us; the launch traced here: 2850 us
  waiting for transfers between devices  2460 us (85%)
  matrix products  155 us (5%)
  local copies, waits for them, and re-layouts  80.6 us (3%)
  blocking collectives  67.3 us (2%)
  other arithmetic  52.8 us (2%)
    reduce_scatter x1, waiting for transfers between devices, on_device(): lax.psum_scatter(partials[10], ('rows', 'seq'), scatter_dimension=0, tile...  667 us
    reduce_scatter x1, waiting for transfers between devices, on_device(): lax.psum_scatter(partials[8], ('rows', 'seq'), scatter_dimension=0, tiled...  666 us
    reduce_scatter x1, waiting for transfers between devices, on_device(): lax.psum_scatter(partials[2], ('rows', 'seq'), scatter_dimension=0, tiled...  658 us
    reduce_scatter x1, waiting for transfers between devices, on_device(): lax.psum_scatter(partials[4], ('rows', 'seq'), scatter_dimension=0, tiled...  369 us
    unnamed x1, blocking collectives  67.3 us
  transfers between devices with their start and end apart: 8, of which 8 were waited for; matrix products, arithmetic and copies ran while one was open for 5% of the time, Pallas kernels for 0%

commit v1 on v0

v1 whole, which is shorter than its diff:
```python
import jax
import jax.numpy as jnp
from jax import lax
from jax.experimental import pallas as pl
from jax.experimental.pallas import tpu as pltpu
from jax.sharding import Mesh, PartitionSpec as P

BF = jnp.bfloat16
F32 = jnp.float32
AXES = ("xh", "y", "c", "xl", "z")
BY_MESH = pl.DeviceIdType.MESH
DIMS = ("x1", "y1", "z1", "x0", "y0", "z0")
UP_GROUPS = ((0, 3, 0), (3, 6, 1), (6, 9, 2), (9, 12, 3), (12, 14, 4), (14, 16, 5))
DOWN_GROUPS = ((0, 1, 0), (1, 2, 1), (2, 3, 2), (3, 4, 3), (4, 6, 4), (6, 8, 5))
OUT_GROUPS = ((0, 1, 0), (1, 2, 1), (2, 3, 2), (3, 4, 3))
BLOCK = 256
GELU = 0.7978845608028654
CUBIC = 0.044715
EPS = 1e-05
MASKED = -1e30
VMEM_LIMIT = 60 * 1024 * 1024


def dot_nn(a, b):
    return lax.dot_general(a, b, (((1,), (0,)), ((), ())), preferred_element_type=F32)


def dot_nt(a, b):
    return lax.dot_general(a, b, (((1,), (1,)), ((), ())), preferred_element_type=F32)


def dot_tn(a, b):
    return lax.dot_general(a, b, (((0,), (0,)), ((), ())), preferred_element_type=F32)


class Place:
    def __init__(self):
        self.xh, self.y, self.c, self.xl, self.z = (lax.axis_index(a) for a in AXES)
        two = jnp.int32(2)
        self.bits = {
            "x1": self.xh,
            "x0": lax.rem(self.xl + self.xh, two),
            "y1": lax.div(self.y, two),
            "y0": lax.rem(self.y + lax.div(self.y, two), two),
            "z1": lax.div(self.z, two),
            "z0": lax.rem(self.z + lax.div(self.z, two), two),
        }

    def partner(self, name):
        xh, y, c, xl, z = self.xh, self.y, self.c, self.xl, self.z
        if name == "c":
            c = 1 - c
        elif name == "x0":
            xl = 1 - xl
        elif name == "x1":
            xh, xl = 1 - xh, 1 - xl
        elif name == "y0":
            y = y + 1 - 2 * lax.rem(y, jnp.int32(2))
        elif name == "y1":
            y = 3 - y
        elif name == "z0":
            z = z + 1 - 2 * lax.rem(z, jnp.int32(2))
        elif name == "z1":
            z = 3 - z
        return (xh, y, c, xl, z)

    def ring(self, axis, step):
        four, two = jnp.int32(4), jnp.int32(2)
        xh, y, c, xl, z = self.xh, self.y, self.c, self.xl, self.z
        if axis == "x":
            at = lax.rem(2 * xh + xl + step, four)
            xh, xl = lax.div(at, two), lax.rem(at, two)
        elif axis == "y":
            y = lax.rem(y + step, four)
        else:
            z = lax.rem(z + step, four)
        return (xh, y, c, xl, z)

    def exchange(self, r):
        return (self.xh, self.y, self.xl, self.c, jnp.int32(r))

    def is_self(self, r):
        return (self.c == self.xl) & (self.z == r)


def order_of(o):
    return DIMS[o:] + DIMS[:o]


def half(n, k):
    return n >> k


def region(k):
    return 64 - (64 >> (k - 1))


def natural_code(s):
    xh, y, xl, z = s >> 5, (s >> 3) & 3, (s >> 2) & 1, s & 3
    bits = (xh, y >> 1, z >> 1, xl ^ xh, (y & 1) ^ (y >> 1), (z & 1) ^ (z >> 1))
    code = 0
    for b in bits:
        code = 2 * code + b
    return code


def turned(code, o):
    return ((code << o) & 63) | (code >> (6 - o))


def turned_by(code, power):
    scaled = code * power
    return lax.rem(scaled, jnp.int32(64)) + lax.div(scaled, jnp.int32(64))


def offset_before(place, o, k):
    off = jnp.int32(0)
    for j, name in enumerate(order_of(o)[: k - 1]):
        off = off + place.bits[name] * (64 >> (j + 1))
    return off


def scatter_copy(place, k, buf, got, lead, o, sends, recvs, at):
    name = order_of(o)[k - 1]
    n = 64 >> k
    start = offset_before(place, o, k) + (1 - place.bits[name]) * n
    return pltpu.make_async_remote_copy(
        src_ref=buf.at[lead + (pl.ds(start, n),)],
        dst_ref=got.at[lead + (pl.ds(region(k), n),)],
        send_sem=sends.at[at],
        recv_sem=recvs.at[at],
        device_id=place.partner(name),
        device_id_type=BY_MESH,
    )


def scatter_add(place, k, buf, got, piece, o):
    n = 64 >> k
    keep = offset_before(place, o, k + 1)
    mine = piece + (pl.ds(keep, n),)
    buf[mine] = buf[mine] + got[piece + (pl.ds(region(k), n),)]


def feature_rows(flat):
    parts = []
    for g in range(8):
        for c in range(2):
            parts.append(flat[(c * 8 + g) * 8 : (c * 8 + g + 1) * 8])
    return jnp.concatenate(parts, axis=0)


def transpose_features(src, dst):
    def body(f, carry):
        block = src[:, pl.ds(pl.multiple_of(f * 128, 128), 128)].astype(F32)
        dst[pl.ds(pl.multiple_of(f * 128, 128), 128), :] = feature_rows(block.T).astype(BF)
        return carry

    lax.fori_loop(0, 8, body, 0)


def norm_parts(v):
    center = v - jnp.mean(v, axis=-1, keepdims=True)
    rstd = lax.rsqrt(jnp.mean(center * center, axis=-1, keepdims=True) + EPS)
    return center * rstd, rstd


def aligned(v, m):
    return pl.multiple_of(v, m)


def window(i):
    return max(0, i - 2) * BLOCK, (i + 1) * BLOCK


def remote(src, dst, send, recv, device):
    return pltpu.make_async_remote_copy(
        src_ref=src, dst_ref=dst, send_sem=send, recv_sem=recv, device_id=device, device_id_type=BY_MESH
    )


def greet(place, devices, with_exchange):
    barrier = pltpu.get_barrier_semaphore()
    count = jnp.int32(len(devices))
    for d in devices:
        pl.semaphore_signal(barrier, inc=1, device_id=d, device_id_type=BY_MESH)
    if with_exchange:
        for r in range(4):

            @pl.when(jnp.logical_not(place.is_self(r)))
            def _(r=r):
                pl.semaphore_signal(barrier, inc=1, device_id=place.exchange(r), device_id_type=BY_MESH)

        count = count + 4 - jnp.where(place.c == place.xl, 1, 0)
    pl.semaphore_wait(barrier, count)


def exchange_start(place, src_of, dst_of, own_dst_of, sends, recvs):
    for r in range(4):
        own = place.is_self(r)

        @pl.when(own)
        def _(r=r):
            pltpu.make_async_copy(src_of(r), own_dst_of(r), recvs.at[place.z]).start()

        @pl.when(jnp.logical_not(own))
        def _(r=r):
            remote(src_of(r), dst_of(r), sends.at[r], recvs.at[place.z], place.exchange(r)).start()


def exchange_sent(place, src_of, dst_of, sends, recvs):
    for r in range(4):

        @pl.when(jnp.logical_not(place.is_self(r)))
        def _(r=r):
            remote(src_of(r), dst_of(r), sends.at[r], recvs.at[place.z], place.exchange(r)).wait_send()


def forward_kernel(
    x_in, c_in, seg_in, flag_in, par, wqkv, wout,
    resid_o, h1_o, c_o, h2_o, qkv_o, ctxp_o, ctxh_o, lse_o, seg_o, x_o,
    wq, wo, seg_got, b0, b1, b2, b3, lse_acc,
    xs, xr, cs, cr, hs, hr, fs, fr, ts, tr, gs, gr, ss, sr, ws,
):
    place = Place()
    c, xl, z = place.c, place.xl, place.z
    mate = place.partner("c")
    loads = [
        pltpu.make_async_copy(
            wqkv.at[:, pl.ds(aligned(j * 1024 + c * 512, 512), 512)], wq.at[:, pl.ds(j * 512, 512)], ws.at[j]
        )
        for j in range(3)
    ]
    loads.append(pltpu.make_async_copy(wout, wo, ws.at[3]))
    for load in loads:
        load.start()
    greet(place, [mate], True)

    def x_src(r):
        return x_in.at[r]

    def x_dst(r):
        return x_o.at[pl.ds(aligned(z * 128, 128), 128)]

    def c_src(r):
        return c_in.at[r]

    def c_dst(r):
        return c_o.at[pl.ds(aligned(xl * 512 + z * 128, 128), 128)]

    exchange_start(place, x_src, x_dst, x_dst, xs, xr)
    seg_out = [remote(ref, seg_got.at[n], ss.at[n], sr.at[n], mate) for n, ref in enumerate((seg_in, flag_in))]
    for copy in seg_out:
        copy.start()
    exchange_start(place, c_src, c_dst, c_dst, cs, cr)

    gain_one, bias_one = par[0:1, :], par[1:2, :]

    def h1_copy(b):
        rows = pl.ds(aligned(c * 512 + b * 128, 128), 128)
        return remote(h1_o.at[rows], h1_o.at[rows], hs.at[b], hr.at[b], mate)

    def c_copy(b):
        rows = pl.ds(aligned(c * 512 + b * 128, 128), 128)
        return remote(c_o.at[rows], c_o.at[rows], fs.at[b], fr.at[b], mate)

    def h1_got(b):
        rows = pl.ds(aligned((1 - c) * 512 + b * 128, 128), 128)
        return remote(h1_o.at[rows], h1_o.at[rows], hs.at[b], hr.at[b], mate)

    def c_got(b):
        rows = pl.ds(aligned((1 - c) * 512 + b * 128, 128), 128)
        return remote(c_o.at[rows], c_o.at[rows], fs.at[b], fr.at[b], mate)

    for b in range(4):
        pltpu.make_async_copy(x_in.at[0], x_o.at[b * 128 : (b + 1) * 128], xr.at[b]).wait()
        xhat, _ = norm_parts(x_o[b * 128 : (b + 1) * 128].astype(F32))
        h1_o[pl.ds(aligned(c * 512 + b * 128, 128), 128)] = (xhat * gain_one + bias_one).astype(BF)
        h1_copy(b).start()

    for copy in seg_out:
        copy.wait()
    own_seg, own_flag = seg_in[pl.ds(z, 1), :], flag_in[pl.ds(z, 1), :]
    far_seg, far_flag = seg_got[0, pl.ds(z, 1), :], seg_got[1, pl.ds(z, 1), :]
    near = jnp.where(c == xl, 1, 0)
    seg_row = jnp.where(near == 1, own_seg, far_seg).astype(F32)
    flag_row = jnp.where(near == 1, own_flag, far_flag)
    key_row = jnp.where(flag_row == 0, seg_row, -1.0)
    seg_o[...] = jnp.concatenate([seg_row, key_row, jnp.zeros((6, 1024), F32)], axis=0)
    seg_col = jnp.broadcast_to(seg_row, (128, 1024)).T
    for i, ref in enumerate((b0, b1, b2, b3)):
        w0, w1 = window(i)
        rows = lax.broadcasted_iota(jnp.int32, (BLOCK, w1 - w0), 0) + i * BLOCK
        cols = lax.broadcasted_iota(jnp.int32, (BLOCK, w1 - w0), 1) + w0
        same = seg_col[i * BLOCK : (i + 1) * BLOCK, 0:1] == key_row[:, w0:w1]
        ref[...] = jnp.where((same & (cols <= rows)) | (rows == cols), 0.0, MASKED)
    lse_acc[...] = jnp.zeros_like(lse_acc)

    for load in loads[:3]:
        load.wait()
    zero = jnp.zeros((1, 512), F32)
    heads = pl.ds(aligned(c * 512, 512), 512)
    bias = jnp.concatenate([par[2:3, heads], zero, par[3:4, heads]], axis=1)

    def project(first):
        def body(n, carry):
            rows = pl.ds(aligned(first + n * BLOCK, BLOCK), BLOCK)
            qkv_o[rows, :] = (dot_nn(h1_o[rows, :], wq[...]) + bias).astype(BF)
            return carry

        lax.fori_loop(0, 2, body, 0)

    project(c * 512)
    for b in range(4):
        h1_got(b).wait_recv()
    project((1 - c) * 512)

    for b in range(4):
        pltpu.make_async_copy(
            c_in.at[0], c_o.at[pl.ds(aligned(c * 512 + b * 128, 128), 128)], cr.at[b]
        ).wait()
        c_copy(b).start()

    lane = lax.broadcasted_iota(jnp.int32, (BLOCK, 128), 1)

    def ctx_copy(p):
        return remote(
            ctxh_o.at[pl.ds(aligned((1 - c) * 512, 512), 512), pl.ds(aligned(p * 128, 128), 128)],
            ctxp_o.at[:, pl.ds(aligned(c * 512 + p * 128, 128), 128)],
            ts.at[p], tr.at[p], mate,
        )

    def attend(p, carry):
        lo = aligned(p * 128, 128)
        for i, ref in enumerate((b0, b1, b2, b3)):
            w0, w1 = window(i)
            rows = slice(i * BLOCK, (i + 1) * BLOCK)
            query = qkv_o[rows, pl.ds(lo, 128)] * jnp.asarray(0.125, BF)
            keys = qkv_o[w0:w1, pl.ds(aligned(512 + lo, 128), 128)]
            values = qkv_o[w0:w1, pl.ds(aligned(1024 + lo, 128), 128)]
            outs = []
            lses = lse_acc[rows, :]
            for h in range(2):
                mine = (lane < 64) if h == 0 else (lane >= 64)
                scores = dot_nt(jnp.where(mine, query, jnp.zeros_like(query)), keys) + ref[...]
                top = jnp.max(scores, axis=-1, keepdims=True)
                expo = jnp.exp(scores - top)
                total = jnp.sum(expo, axis=-1, keepdims=True)
                outs.append(dot_nn(expo.astype(BF), values) * (1.0 / total))
                lses = jnp.where(lane == 2 * p + h, top + jnp.log(total), lses)
            lse_acc[rows, :] = lses
            ctxh_o[rows, pl.ds(lo, 128)] = jnp.where(lane < 64, outs[0], outs[1]).astype(BF)
        ctx_copy(p).start()
        ctxp_o[:, pl.ds(aligned(c * 512 + lo, 128), 128)] = ctxh_o[pl.ds(aligned(c * 512, 512), 512), pl.ds(lo, 128)]
        return carry

    lax.fori_loop(0, 4, attend, 0)
    lse_o[...] = lse_acc[...].T[0:16, :]

    loads[3].wait()
    for p in range(4):
        remote(
            ctxh_o.at[pl.ds(aligned((1 - c) * 512, 512), 512), pl.ds(p * 128, 128)],
            ctxp_o.at[:, pl.ds(aligned((1 - c) * 512 + p * 128, 128), 128)],
            ts.at[p], tr.at[p], mate,
        ).wait_recv()

    def h2_copy(n):
        rows = pl.ds(aligned(c * 512 + n * BLOCK, BLOCK), BLOCK)
        return remote(h2_o.at[rows], h2_o.at[rows], gs.at[n], gr.at[n], mate)

    def h2_got(n):
        rows = pl.ds(aligned((1 - c) * 512 + n * BLOCK, BLOCK), BLOCK)
        return remote(h2_o.at[rows], h2_o.at[rows], gs.at[n], gr.at[n], mate)

    def output(n, carry):
        rows = pl.ds(aligned(n * BLOCK, BLOCK), BLOCK)
        resid = x_o[rows, :].astype(F32) + (dot_nn(ctxp_o[rows, :], wo[...]) + par[4:5, :])
        resid_o[rows, :] = resid
        xhat, _ = norm_parts(resid)
        h2_o[pl.ds(aligned(c * 512 + n * BLOCK, BLOCK), BLOCK), :] = (xhat * par[5:6, :] + par[6:7, :]).astype(BF)
        h2_copy(n).start()
        return carry

    lax.fori_loop(0, 2, output, 0)

    exchange_sent(place, x_src, x_dst, xs, xr)
    exchange_sent(place, c_src, c_dst, cs, cr)
    for b in range(4):
        h1_copy(b).wait_send()
        c_copy(b).wait_send()
        c_got(b).wait_recv()
        ctx_copy(b).wait_send()
    for n in range(2):
        h2_copy(n).wait_send()
        h2_got(n).wait_recv()


def vmem(n=None):
    return pl.BlockSpec(memory_space=pltpu.VMEM)


def anywhere():
    return pl.BlockSpec(memory_space=pl.ANY)


def dma(*shape):
    return pltpu.SemaphoreType.DMA(shape)


def shaped(shape, dtype):
    return jax.ShapeDtypeStruct(shape, dtype)


def run_forward(x, cot, seg, flags, par, wqkv, wout):
    outs = (
        shaped((512, 1024), F32), shaped((1024, 1024), BF), shaped((1024, 1024), BF), shaped((1024, 1024), BF),
        shaped((1024, 1536), BF), shaped((512, 1024), BF), shaped((1024, 512), BF), shaped((16, 1024), F32),
        shaped((8, 1024), F32), shaped((512, 1024), BF),
    )
    return pl.pallas_call(
        forward_kernel,
        out_shape=outs,
        in_specs=[anywhere(), anywhere(), vmem(), vmem(), vmem(), anywhere(), anywhere()],
        out_specs=tuple(vmem() for _ in outs),
        scratch_shapes=[
            pltpu.VMEM((1024, 1536), BF), pltpu.VMEM((1024, 1024), BF), pltpu.VMEM((2, 4, 1024), jnp.int32),
            pltpu.VMEM((256, 256), F32), pltpu.VMEM((256, 512), F32), pltpu.VMEM((256, 768), F32),
            pltpu.VMEM((256, 768), F32), pltpu.VMEM((1024, 128), F32),
            dma(4), dma(4), dma(4), dma(4), dma(4), dma(4), dma(4), dma(4), dma(4), dma(4), dma(2), dma(2), dma(2),
            dma(2), dma(4),
        ],
        compiler_params=pltpu.CompilerParams(collective_id=0, has_side_effects=True, vmem_limit_bytes=VMEM_LIMIT),
        name="forward",
    )(x, cot, seg, flags, par, wqkv, wout)


def middle_kernel(
    h2, cot, resid, ctxp, par, wup, wdown, wout,
    lout_o, dres_o, dctx_o, bup_o, bdown_o, bout_o, small_o,
    wu, wd, h2t, act_s, dup_s, down_acc, dh_acc, dh_send, dh_got, dn_send, dn_got, wo_send, wo_got, dc_send, ctxt, dat,
    us, ds, es, er,
):
    place = Place()
    c = place.c
    mate = place.partner("c")

    def up_load(t):
        return pltpu.make_async_copy(
            wup.at[:, pl.ds(aligned((2 * t + c) * 256, 256), 256)], wu.at[t], us.at[t]
        )

    def down_load(t):
        return pltpu.make_async_copy(wdown.at[pl.ds(aligned((2 * t + c) * 256, 256), 256)], wd.at[t], ds.at[t])

    for t in range(8):
        up_load(t).start()
        down_load(t).start()
    greet(place, [mate], False)

    transpose_features(h2, h2t)
    small_o[...] = jnp.zeros_like(small_o)

    def tile(t, carry):
        up_load(t).wait()
        down_load(t).wait()
        col = 2 * t + c
        up_bias = par[pl.ds(8 + lax.div(col, jnp.int32(4)), 1), pl.ds(aligned(lax.rem(col, jnp.int32(4)) * 256, 256), 256)]
        dbias = jnp.zeros((1, 256), F32)
        for b in range(4):
            rows = slice(b * BLOCK, (b + 1) * BLOCK)
            u = dot_nn(h2[rows, :], wu[t]) + up_bias
            dact = dot_nt(cot[rows, :], wd[t])
            square = u * u
            th = jnp.tanh(GELU * u * (1.0 + CUBIC * square))
            act_s[rows, :] = (0.5 * u * (1.0 + th)).astype(BF)
            slope = 0.5 * (1.0 + th) + 0.5 * u * (1.0 - th * th) * (GELU * (1.0 + (3.0 * CUBIC) * square))
            dup = (dact * slope).astype(BF)
            dup_s[rows, :] = dup
            dbias = dbias + jnp.sum(dup.astype(F32), axis=0, keepdims=True)
        small_o[pl.ds(8 + lax.div(col, jnp.int32(4)), 1), pl.ds(aligned(lax.rem(col, jnp.int32(4)) * 256, 256), 256)] = dbias

        xh, y = lax.div(t, jnp.int32(4)), lax.rem(t, jnp.int32(4))
        y1 = lax.div(y, jnp.int32(2))
        y0 = lax.rem(y + y1, jnp.int32(2))
        grad = dot_tn(act_s[...], cot[...]).astype(BF)
        for s in range(8):
            sx, sz = s >> 2, s & 3
            x0 = lax.rem(xh + sx, jnp.int32(2))
            code = xh * 32 + y1 * 16 + (sz >> 1) * 8 + x0 * 4 + y0 * 2 + ((sz & 1) ^ (sz >> 1))
            for p0, p1, o in DOWN_GROUPS:
                slot = turned_by(code, 1 << o)
                for j in range(p0, p1):
                    bdown_o[j, slot] = grad[s * 32 : (s + 1) * 32, j * 128 : (j + 1) * 128]

        powers = []
        for j in range(2):
            p = 2 * t + j
            o = lax.div(p, jnp.int32(3)) + lax.div(p, jnp.int32(14)) - lax.div(p, jnp.int32(15))
            powers.append(lax.shift_left(jnp.int32(1), o))
        for b in range(4):
            grad = dot_nn(h2t[b * 256 : (b + 1) * 256, :], dup_s[...]).astype(BF)
            for s in range(16):
                code = natural_code(b * 16 + s)
                for j in range(2):
                    bup_o[2 * t + j, turned_by(jnp.int32(code), powers[j])] = grad[
                        s * 16 : (s + 1) * 16, j * 128 : (j + 1) * 128
                    ]

        @pl.when(t == 0)
        def _():
            for b in range(4):
                rows = slice(b * BLOCK, (b + 1) * BLOCK)
                down_acc[rows, :] = dot_nn(act_s[rows, :], wd[t])
                dh_acc[rows, :] = dot_nt(dup_s[rows, :], wu[t])

        @pl.when(t > 0)
        def _():
            for b in range(4):
                rows = slice(b * BLOCK, (b + 1) * BLOCK)
                down_acc[rows, :] = down_acc[rows, :] + dot_nn(act_s[rows, :], wd[t])
                dh_acc[rows, :] = dh_acc[rows, :] + dot_nt(dup_s[rows, :], wu[t])

        return carry

    lax.fori_loop(0, 8, tile, 0)

    own = pl.ds(aligned(c * 512, 512), 512)
    far = pl.ds(aligned((1 - c) * 512, 512), 512)
    dh_send[...] = dh_acc[far, :].astype(BF)
    dh_copy = remote(dh_send, dh_got, es.at[0], er.at[0], mate)
    dh_copy.start()
    dn_send[...] = down_acc[far, :].astype(BF)
    dn_copy = remote(dn_send, dn_got, es.at[1], er.at[1], mate)
    dn_copy.start()

    transpose_features(ctxp, ctxt)

    dh_copy.wait()

    def norm_back(n, sums):
        gain_sum, bias_sum, out_sum, down_sum = sums
        rows = pl.ds(aligned(n * 128, 128), 128)
        mine = pl.ds(aligned(c * 512 + n * 128, 128), 128)
        xhat, rstd = norm_parts(resid[rows, :])
        dn = dh_acc[mine, :] + dh_got[rows, :].astype(F32)
        e = dn * par[5:6, :]
        cf = cot[mine, :].astype(F32)
        dres = cf + rstd * (
            e - jnp.mean(e, axis=-1, keepdims=True) - xhat * jnp.mean(e * xhat, axis=-1, keepdims=True)
        )
        dres_o[rows, :] = dres
        low = dres.astype(BF)
        dat[rows, :] = low
        return (
            gain_sum + jnp.sum(dn * xhat, axis=0, keepdims=True),
            bias_sum + jnp.sum(dn, axis=0, keepdims=True),
            out_sum + jnp.sum(low.astype(F32), axis=0, keepdims=True),
            down_sum + jnp.sum(cf, axis=0, keepdims=True),
        )

    nothing = jnp.zeros((1, 1024), F32)
    gain_sum, bias_sum, out_sum, down_sum = lax.fori_loop(0, 4, norm_back, (nothing,) * 4)
    small_o[5:6, :] = gain_sum
    small_o[6:7, :] = bias_sum
    small_o[4:5, :] = out_sum
    small_o[7:8, :] = down_sum

    dc_send[...] = dot_nt(dat[...], wout[far, :]).astype(BF)
    dc_copy = remote(dc_send, dctx_o.at[own], es.at[2], er.at[2], mate)
    dc_copy.start()

    def out_grad(cols, dst):
        for b in range(4):
            grad = dot_nn(ctxt[b * 256 : (b + 1) * 256, :], dat[:, cols]).astype(BF)
            for s in range(16):
                code = natural_code(b * 16 + s)
                for j in range(4):
                    dst[j, turned(code, j)] = grad[s * 16 : (s + 1) * 16, j * 128 : (j + 1) * 128]

    out_grad(far, wo_send)
    wo_copy = remote(wo_send, wo_got, es.at[3], er.at[3], mate)
    wo_copy.start()
    dctx_o[own, :] = dot_nt(dat[...], wout[own, :]).astype(BF)
    out_grad(own, bout_o)
    dn_copy.wait()
    for n in range(4):
        rows = slice(n * 128, (n + 1) * 128)
        mine = pl.ds(aligned(c * 512 + n * 128, 128), 128)
        down = down_acc[mine, :] + dn_got[rows, :].astype(F32) + par[7:8, :]
        lout_o[rows, :] = (resid[rows, :] + down).astype(BF)
    wo_copy.wait()
    bout_o[...] = bout_o[...] + wo_got[...]
    dc_copy.wait_send()
    remote(dc_send, dctx_o.at[far], es.at[2], er.at[2], mate).wait_recv()


def run_middle(h2, cot, resid, ctxp, par, wup, wdown, wout):
    outs = (
        shaped((512, 1024), BF), shaped((512, 1024), F32), shaped((1024, 512), BF), shaped((16, 64, 16, 128), BF),
        shaped((8, 64, 32, 128), BF), shaped((4, 64, 16, 128), BF), shaped((16, 1024), F32),
    )
    return pl.pallas_call(
        middle_kernel,
        out_shape=outs,
        in_specs=[vmem(), vmem(), vmem(), vmem(), vmem(), anywhere(), anywhere(), vmem()],
        out_specs=tuple(vmem() for _ in outs),
        scratch_shapes=[
            pltpu.VMEM((8, 1024, 256), BF), pltpu.VMEM((8, 256, 1024), BF), pltpu.VMEM((1024, 1024), BF),
            pltpu.VMEM((1024, 256), BF), pltpu.VMEM((1024, 256), BF), pltpu.VMEM((1024, 1024), F32),
            pltpu.VMEM((1024, 1024), F32), pltpu.VMEM((512, 1024), BF), pltpu.VMEM((512, 1024), BF),
            pltpu.VMEM((512, 1024), BF), pltpu.VMEM((512, 1024), BF), pltpu.VMEM((4, 64, 16, 128), BF),
            pltpu.VMEM((4, 64, 16, 128), BF), pltpu.VMEM((512, 512), BF), pltpu.VMEM((1024, 512), BF),
            pltpu.VMEM((512, 1024), BF), dma(8), dma(8), dma(4), dma(4),
        ],
        compiler_params=pltpu.CompilerParams(collective_id=1, has_side_effects=True, vmem_limit_bytes=VMEM_LIMIT),
        name="middle",
    )(h2, cot, resid, ctxp, par, wup, wdown, wout)


MAIN = tuple(
    (which, p0, p1, o)
    for which, groups in ((0, UP_GROUPS), (1, DOWN_GROUPS), (2, OUT_GROUPS))
    for p0, p1, o in groups
)
EVENTS = {(1, 3): 1, (2, 1): 2, (2, 3): 3, (3, 0): 4, (3, 1): 5, (3, 2): 6}


def backward_kernel(
    qkv, dctx, ctxh, lse, seg, h1, x_own, dres, small_in, par, lout, bup_in, bdown_in, bout_in, wqkv,
    lout_o, gin_o, gqkv_o, gout_o, gup_o, gdown_o, small_o,
    wq, h1t, dqkv, dk_acc, dv_acc, drow, t0, t1, t2, t3, bup, bdown, bout, bqkv, rup, rdown, rout, rqkv,
    fin_up, fin_out, fin_qkv, far_up, far_out, far_qkv, dh_send, dh_got, dh_own, gin_s,
    sm, sm_first, sm_acc, sm_got, sm_last,
    ws, ms, mr, q1s, q1r, qs, qr, ls, lr, gs, gr, es, er, ps, pr,
):
    place = Place()
    c, xl, z = place.c, place.xl, place.z
    mate = place.partner("c")
    loads = [
        pltpu.make_async_copy(bup_in, bup, ws.at[0]),
        pltpu.make_async_copy(bdown_in, bdown, ws.at[1]),
        pltpu.make_async_copy(bout_in, bout, ws.at[2]),
    ]
    for p in range(4):
        for j in range(3):
            loads.append(
                pltpu.make_async_copy(
                    wqkv.at[:, pl.ds(aligned(j * 1024 + c * 512 + p * 128, 128), 128)],
                    wq.at[:, pl.ds(p * 384 + j * 128, 128)],
                    ws.at[3 + p * 3 + j],
                )
            )
    for load in loads:
        load.start()
    peers = [mate] + [place.partner(d) for d in DIMS] + [place.ring(a, s) for a in "xyz" for s in (1, 2, 3)]
    greet(place, peers, True)

    def l_src(r):
        return lout.at[pl.ds(r * 128, 128)]

    def l_dst(r):
        return lout_o.at[z]

    exchange_start(place, l_src, l_dst, l_dst, ls, lr)
    for load in loads[:3]:
        load.wait()
    bufs, gots = (bup, bdown, bout), (rup, rdown, rout)

    def main_copy(k, n):
        which, p0, p1, o = MAIN[n]
        return scatter_copy(place, k, bufs[which], gots[which], (slice(p0, p1),), o, ms, mr, (k - 1, n))

    def main_start(k):
        for n in range(len(MAIN)):
            main_copy(k, n).start()

    def main_finish(k):
        for n in range(len(MAIN)):
            main_copy(k, n).wait()
        if k < 6:
            for which, p0, p1, o in MAIN:
                for p in range(p0, p1):
                    scatter_add(place, k, bufs[which], gots[which], (p,), o)

    main_start(1)

    key_col = jnp.broadcast_to(seg[1:2, :], (128, 1024)).T
    for i, ref in enumerate((t0, t1, t2, t3)):
        w0, w1 = window(i)
        rows = lax.broadcasted_iota(jnp.int32, (w1 - w0, BLOCK), 0) + w0
        cols = lax.broadcasted_iota(jnp.int32, (w1 - w0, BLOCK), 1) + i * BLOCK
        same = key_col[w0:w1, 0:1] == seg[0:1, i * BLOCK : (i + 1) * BLOCK]
        ref[...] = jnp.where((same & (rows <= cols)) | (rows == cols), 0.0, MASKED)
    transpose_features(h1, h1t)
    sm[...] = small_in[...]

    lane = lax.broadcasted_iota(jnp.int32, (BLOCK, 128), 1)
    head_of = lax.broadcasted_iota(jnp.int32, (16, 128), 1)
    row_of = lax.broadcasted_iota(jnp.int32, (16, 128), 0)
    pick = jnp.where(lax.div(head_of, jnp.int32(64)) == row_of, 1.0, 0.0).astype(BF)

    def final_sum(buf, got, piece, o):
        off = offset_before(place, o, 7)
        return buf[piece, off].astype(F32) + got[piece, 62].astype(F32)

    def far_rows(n):
        return pl.ds(aligned((1 - c) * 8, 8), 8)

    def far_copy(src, dst, at):
        return remote(src.at[pl.ds(aligned((1 - c) * 8, 8), 8)], dst, es.at[at], er.at[at], mate)

    def main_last():
        for p0, p1, o in UP_GROUPS:
            for p in range(p0, p1):
                fin_up[:, p * 128 : (p + 1) * 128] = final_sum(bup, rup, p, o)
        far_copy(fin_up, far_up, 0).start()
        for p0, p1, o in OUT_GROUPS:
            fin_out[:, p0 * 128 : (p0 + 1) * 128] = final_sum(bout, rout, p0, o)
        far_copy(fin_out, far_out, 1).start()
        for p0, p1, o in DOWN_GROUPS:
            for p in range(p0, p1):
                gdown_o[:, p * 128 : (p + 1) * 128] = final_sum(bdown, rdown, p, o)

    def first_copy(p, j):
        o = (3 * p + j) % 6
        return scatter_copy(place, 1, bqkv, rqkv, (o, p // 2), o, q1s, q1r, p * 3 + j)

    def pair(p, carry):
        lo = aligned(p * 128, 128)
        prod = (dctx[:, pl.ds(lo, 128)].astype(F32) * ctxh[:, pl.ds(lo, 128)].astype(F32)).astype(BF)
        drow[...] = dot_nt(pick, prod)
        dk_acc[...] = jnp.zeros_like(dk_acc)
        dv_acc[...] = jnp.zeros_like(dv_acc)
        at = p * 384
        for i, ref in enumerate((t0, t1, t2, t3)):
            w0, w1 = window(i)
            rows = slice(i * BLOCK, (i + 1) * BLOCK)
            query = qkv[rows, pl.ds(lo, 128)] * jnp.asarray(0.125, BF)
            keys = qkv[w0:w1, pl.ds(aligned(512 + lo, 128), 128)]
            values = qkv[w0:w1, pl.ds(aligned(1024 + lo, 128), 128)]
            grad = dctx[rows, pl.ds(lo, 128)]
            dq = []
            for h in range(2):
                mine = (lane < 64) if h == 0 else (lane >= 64)
                query_h = jnp.where(mine, query, jnp.zeros_like(query))
                grad_h = jnp.where(mine, grad, jnp.zeros_like(grad))
                scores = dot_nt(keys, query_h) + ref[...]
                probs = jnp.exp(scores - lse[pl.ds(2 * p + h, 1), rows])
                dprobs = dot_nt(values, grad_h)
                dscores = (probs * (dprobs - drow[h : h + 1, rows])).astype(BF)
                dv_acc[w0:w1, :] = dv_acc[w0:w1, :] + dot_nn(probs.astype(BF), grad_h)
                dk_acc[w0:w1, :] = dk_acc[w0:w1, :] + dot_nn(dscores, query_h)
                dq.append(dot_tn(dscores, keys))
            dqkv[rows, pl.ds(aligned(at, 128), 128)] = (jnp.where(lane < 64, dq[0], dq[1]) * 0.125).astype(BF)
            for (ep, ei), k in EVENTS.items():
                if ei == i:

                    @pl.when(p == ep)
                    def _(k=k):
                        main_finish(k)
                        if k < 6:
                            main_start(k + 1)
                        else:
                            main_last()

        dqkv[:, pl.ds(aligned(at + 128, 128), 128)] = dk_acc[...].astype(BF)
        dqkv[:, pl.ds(aligned(at + 256, 128), 128)] = dv_acc[...].astype(BF)
        own = pl.ds(aligned(c * 512 + lo, 128), 128)
        sm[2:3, own] = jnp.sum(dqkv[:, pl.ds(aligned(at, 128), 128)].astype(F32), axis=0, keepdims=True)
        sm[3:4, own] = jnp.sum(dqkv[:, pl.ds(aligned(at + 256, 128), 128)].astype(F32), axis=0, keepdims=True)
        base = 3 * lax.rem(p, jnp.int32(2))
        powers = [lax.shift_left(jnp.int32(1), base + j) for j in range(3)]
        for b in range(4):
            grad = dot_nn(h1t[b * 256 : (b + 1) * 256, :], dqkv[:, pl.ds(aligned(at, 128), 384)]).astype(BF)
            for s in range(16):
                code = natural_code(b * 16 + s)
                for j in range(3):
                    bqkv[base + j, lax.div(p, jnp.int32(2)), turned_by(jnp.int32(code), powers[j])] = grad[
                        s * 16 : (s + 1) * 16, j * 128 : (j + 1) * 128
                    ]
        for q in range(4):

            @pl.when(p == q)
            def _(q=q):
                for j in range(3):
                    first_copy(q, j).start()

        return carry

    lax.fori_loop(0, 4, pair, 0)

    def rest_copy(k, o):
        return scatter_copy(place, k, bqkv, rqkv, (o, slice(0, 2)), o, qs, qr, (k - 2, o))

    def rest_add(k):
        for o in range(6):
            for m in range(2):
                scatter_add(place, k, bqkv, rqkv, (o, m), o)

    def rest_start(k):
        for o in range(6):
            rest_copy(k, o).start()

    def rest_finish(k):
        for o in range(6):
            rest_copy(k, o).wait()

    for q in range(4):
        for j in range(3):
            first_copy(q, j).wait()
    rest_add(1)
    rest_start(2)

    for load in loads[3:]:
        load.wait()
    dh_copy = remote(dh_send, dh_got, es.at[2], er.at[2], mate)

    def far_half(n, carry):
        rows = pl.ds(aligned((1 - c) * 512 + n * BLOCK, BLOCK), BLOCK)
        dh_send[pl.ds(aligned(n * BLOCK, BLOCK), BLOCK), :] = dot_nt(dqkv[rows, :], wq[...]).astype(BF)
        return carry

    lax.fori_loop(0, 2, far_half, 0)
    dh_copy.start()
    rest_finish(2)
    rest_add(2)
    rest_start(3)

    def own_half(n, carry):
        rows = pl.ds(aligned(c * 512 + n * BLOCK, BLOCK), BLOCK)
        dh_own[pl.ds(aligned(n * BLOCK, BLOCK), BLOCK), :] = dot_nt(dqkv[rows, :], wq[...])
        return carry

    lax.fori_loop(0, 2, own_half, 0)
    rest_finish(3)
    rest_add(3)
    rest_start(4)
    dh_copy.wait()

    def norm_back(n, sums):
        gain_sum, bias_sum = sums
        rows = pl.ds(aligned(n * 128, 128), 128)
        xhat, rstd = norm_parts(x_own[rows, :].astype(F32))
        dn = dh_own[rows, :] + dh_got[rows, :].astype(F32)
        e = dn * par[0:1, :]
        gin_s[rows, :] = (
            dres[rows, :]
            + rstd * (e - jnp.mean(e, axis=-1, keepdims=True) - xhat * jnp.mean(e * xhat, axis=-1, keepdims=True))
        ).astype(BF)
        return (
            gain_sum + jnp.sum(dn * xhat, axis=0, keepdims=True),
            bias_sum + jnp.sum(dn, axis=0, keepdims=True),
        )

    nothing = jnp.zeros((1, 1024), F32)
    gain_sum, bias_sum = lax.fori_loop(0, 4, norm_back, (nothing,) * 2)
    sm[0:1, :] = gain_sum
    sm[1:2, :] = bias_sum

    own8 = pl.ds(aligned(c * 8, 8), 8)
    far8 = pl.ds(aligned((1 - c) * 8, 8), 8)
    small_copy = remote(sm.at[far8], sm_first, es.at[3], er.at[3], mate)
    small_copy.start()

    def g_src(r):
        return gin_s.at[pl.ds(r * 128, 128)]

    def g_dst(r):
        return gin_o.at[z]

    exchange_start(place, g_src, g_dst, g_dst, gs, gr)
    rest_finish(4)
    rest_add(4)
    rest_start(5)

    small_copy.wait()
    sm_acc[0] = sm[own8, :] + sm_first[...]

    def phase_copy(n, s):
        return remote(sm_acc.at[n], sm_got.at[n, s - 1], ps.at[n, s - 1], pr.at[n, s - 1], place.ring("zyx"[n], s))

    for n in range(3):
        for s in (1, 2, 3):
            phase_copy(n, s).start()
        if n < 2:
            rest_finish(5 + n)
            if n == 0:
                rest_add(5)
                rest_start(6)
            else:
                for o in range(6):
                    for m in range(2):
                        p, j = 2 * m + o // 3, o % 3
                        off = offset_before(place, o, 7)
                        fin_qkv[:, j * 512 + p * 128 : j * 512 + (p + 1) * 128] = bqkv[o, m, off].astype(F32) + rqkv[
                            o, m, 62
                        ].astype(F32)
                far_copy(fin_qkv, far_qkv, 4).start()
        for s in (1, 2, 3):
            phase_copy(n, s).wait()
        sm_acc[n + 1] = sm_acc[n] + sm_got[n, 0] + sm_got[n, 1] + sm_got[n, 2]

    last_copy = remote(sm_acc.at[3], sm_last, es.at[5], er.at[5], mate)
    last_copy.start()

    own8 = pl.ds(aligned(c * 8, 8), 8)
    far_copy(fin_up, far_up, 0).wait()
    for t in range(8):
        mine, theirs = fin_up[own8, t * 256 : (t + 1) * 256], far_up[:, t * 256 : (t + 1) * 256]
        gup_o[:, t * 512 : t * 512 + 256] = jnp.where(c == 0, mine, theirs)
        gup_o[:, t * 512 + 256 : t * 512 + 512] = jnp.where(c == 0, theirs, mine)
    far_copy(fin_out, far_out, 1).wait()
    mine, theirs = fin_out[own8, :], far_out[...]
    gout_o[:, 0:512] = jnp.where(c == 0, mine, theirs)
    gout_o[:, 512:1024] = jnp.where(c == 0, theirs, mine)
    far_copy(fin_qkv, far_qkv, 4).wait()
    for j in range(3):
        mine, theirs = fin_qkv[own8, j * 512 : (j + 1) * 512], far_qkv[:, j * 512 : (j + 1) * 512]
        gqkv_o[:, j * 1024 : j * 1024 + 512] = jnp.where(c == 0, mine, theirs)
        gqkv_o[:, j * 1024 + 512 : j * 1024 + 1024] = jnp.where(c == 0, theirs, mine)
    last_copy.wait()
    mine, theirs = sm_acc[3], sm_last[...]
    small_o[0:8, :] = jnp.where(c == 0, mine, theirs)
    small_o[8:16, :] = jnp.where(c == 0, theirs, mine)

    exchange_sent(place, l_src, l_dst, ls, lr)
    exchange_sent(place, g_src, g_dst, gs, gr)
    for b in range(4):
        pltpu.make_async_copy(lout.at[pl.ds(0, 128)], lout_o.at[b], lr.at[b]).wait()
        pltpu.make_async_copy(gin_s.at[pl.ds(0, 128)], gin_o.at[b], gr.at[b]).wait()


def run_backward(*args):
    outs = (
        shaped((4, 128, 1024), BF), shaped((4, 128, 1024), BF), shaped((8, 3072), F32), shaped((8, 1024), F32),
        shaped((8, 4096), F32), shaped((32, 1024), F32), shaped((16, 1024), F32),
    )
    v = pltpu.VMEM
    return pl.pallas_call(
        backward_kernel,
        out_shape=outs,
        in_specs=[vmem()] * 10 + [anywhere()] * 5,
        out_specs=(anywhere(), anywhere()) + (vmem(),) * 5,
        scratch_shapes=[
            v((1024, 1536), BF), v((1024, 1024), BF), v((1024, 1536), BF), v((1024, 128), F32), v((1024, 128), F32),
            v((16, 1024), F32), v((256, 256), F32), v((512, 256), F32), v((768, 256), F32), v((768, 256), F32),
            v((16, 64, 16, 128), BF), v((8, 64, 32, 128), BF), v((4, 64, 16, 128), BF), v((6, 2, 64, 16, 128), BF),
            v((16, 63, 16, 128), BF), v((8, 63, 32, 128), BF), v((4, 63, 16, 128), BF), v((6, 2, 63, 16, 128), BF),
            v((16, 2048), F32), v((16, 512), F32), v((16, 1536), F32), v((8, 2048), F32), v((8, 512), F32),
            v((8, 1536), F32), v((512, 1024), BF), v((512, 1024), BF), v((512, 1024), F32), v((512, 1024), BF),
            v((16, 1024), F32), v((8, 1024), F32), v((4, 8, 1024), F32), v((3, 3, 8, 1024), F32), v((8, 1024), F32),
            dma(15), dma(6, 16), dma(6, 16), dma(12), dma(12), dma(5, 6), dma(5, 6), dma(4), dma(4), dma(4), dma(4),
            dma(6), dma(6), dma(3, 3), dma(3, 3),
        ],
        compiler_params=pltpu.CompilerParams(collective_id=2, has_side_effects=True, vmem_limit_bytes=VMEM_LIMIT),
        name="backward",
    )(*args)


def on_device(
    block_input, segment_ids, padding_flags, cotangent, norm_one_gain, norm_one_bias, query_key_value, query_value_bias,
    out_weight, out_bias, norm_two_gain, norm_two_bias, up_weight, up_bias, down_weight, down_bias,
):
    par = jnp.concatenate(
        [
            norm_one_gain, norm_one_bias, query_value_bias, out_bias, norm_two_gain, norm_two_bias, down_bias, up_bias,
            jnp.zeros((4096,), BF),
        ]
    ).astype(F32).reshape(16, 1024)
    resid, h1, cot, h2, qkv, ctxp, ctxh, lse, seg, x_own = run_forward(
        block_input, cotangent, segment_ids, padding_flags, par, query_key_value, out_weight
    )
    lout, dres, dctx, bup, bdown, bout, small = run_middle(h2, cot, resid, ctxp, par, up_weight, down_weight, out_weight)
    lout, gin, gqkv, gout, gup, gdown, sums = run_backward(
        qkv, dctx, ctxh, lse, seg, h1, x_own, dres, small, par, lout, bup, bdown, bout, query_key_value
    )
    device = ((lax.axis_index("xh") * 4 + lax.axis_index("y")) * 2 + lax.axis_index("c")) * 8
    device = device + lax.axis_index("xl") * 4 + lax.axis_index("z")
    flat = sums.reshape(16 * 1024)

    def part(first, size):
        return lax.dynamic_slice(flat, (first * 1024 + device * size,), (size,))

    return (
        lout, gin, part(0, 8), part(1, 8), gqkv, part(2, 16), gout, part(4, 8), part(5, 8), part(6, 8), gup,
        part(8, 32), gdown, part(7, 8),
    )


def solution(mesh):
    wide = Mesh(mesh.devices.reshape(2, 4, 2, 2, 4), AXES)
    rows, seq = ("xh", "y", "c"), ("xl", "z")
    everything = rows + seq
    whole = P()
    return jax.shard_map(
        on_device,
        mesh=wide,
        in_specs=(P(rows, seq, None), P(rows, None), P(rows, None), P(rows, seq, None)) + (whole,) * 12,
        out_specs=(
            P(rows, seq, None), P(rows, seq, None), P(everything), P(everything), P(everything, None), P(everything),
            P(everything, None), P(everything), P(everything), P(everything), P(everything, None), P(everything),
            P(everything, None), P(everything),
        ),
        check_vma=False,
    )
```

time: 2880 us -> 261 us (0.09)
  waiting for transfers between devices: 2460 us -> 0 us
  Pallas kernels: 0 us -> 243 us
  matrix products: 155 us -> 0 us
  blocking collectives: 67.3 us -> 0 us
  local copies, waits for them, and re-layouts: 80.6 us -> 16 us
  other arithmetic: 52.8 us -> 0 us
    reduce_scatter x4 -> x0, waiting for transfers between devices: 2360 us -> none  [the longest x1 667 us: on_device(): lax.psum_scatter(partials[10], ('rows', 'seq'), scatter_dimension=0, tile...]
    pallas_call x0 -> x3, Pallas kernels: none -> 243 us  [the longest x1 134 us: run_backward(): pl.pallas_call(backward_kernel, out_shape=outs, in_specs=[vmem()] * 10 +...]
    dot_general x40 -> x0, matrix products: 155 us -> none  [the longest x4 37.4 us: contract_rows(): lax.dot_general(left, right, (((0,), (0,)), ((), ())), preferred_element_...]
    all_to_all x4 -> x0, waiting for transfers between devices: 102 us -> none  [the longest x1 38.1 us: on_device(): lax.all_to_all(grad_qkv_heads, 'seq', split_axis=1, concat_axis=3, tiled=...]
    unnamed x1 -> x0, blocking collectives: 67.3 us -> none
  transfers between devices with their start and end apart: 8 -> 0, of which waited for: 8 -> 0; matrix products, arithmetic and copies ran while one was open for 5% -> 0% of each run, Pallas kernels for 0% -> 0%
where the time goes in v1:
time: 261 us; the launch traced here: 260 us
  Pallas kernels  243 us (93%)
  local copies, waits for them, and re-layouts  16 us (6%)
    pallas_call x1, Pallas kernels, run_backward(): pl.pallas_call(backward_kernel, out_shape=outs, in_specs=[vmem()] * 10 +...  134 us
    pallas_call x1, Pallas kernels, run_middle(): pl.pallas_call(middle_kernel, out_shape=outs, in_specs=[vmem(), vmem(), v...  55.3 us
    pallas_call x1, Pallas kernels, run_forward(): pl.pallas_call(forward_kernel, out_shape=outs, in_specs=[anywhere(), anyw...  53.9 us
    unnamed x23, local copies, waits for them, and re-layouts  13.5 us

profile of v1, /device:TPU:1, one launch (start us, length us, event | category | flops | bytes accessed | tf_op | source)
XLA Modules:
  0.0 260.0 jit_solution(4014049045492657291)
XLA Ops:
  0.6 0.7 constant_dynamic-update-slice_fusion.8
  1.3 0.7 constant_dynamic-update-slice_fusion.7
  2.0 0.7 constant_dynamic-update-slice_fusion.6
  2.7 0.7 constant_dynamic-update-slice_fusion.5
  3.4 0.7 constant_dynamic-update-slice_fusion.4
  4.1 0.7 constant_dynamic-update-slice_fusion.3
  4.8 0.7 constant_dynamic-update-slice_fusion.2
  5.5 0.7 constant_dynamic-update-slice_fusion.1
  6.2 0.6 reshape.36.par
  6.8 53.9 %forward.1 = (f32[512,1024]{1,0:T(8,128)}, bf16[1024,1024]{1,0:T(8,128)(2,1)}, bf16[1024,1024]{1,0:T(8,128)(2,1)}, bf16[1024,1024]{1,0:T(8,128)(2,1)}, bf16[1024...) custom-call(bf16[4,128,1024]{2,1,0:T(8,128)(2,1)} %x_in.1, ...), custom_call_target="tpu_custom_call" | custom-call | tf_op jit(solution)/shard_map/forward/pallas_call | solution.py:420
  60.7 55.3 %middle.1 = (bf16[512,1024]{1,0:T(8,128)(2,1)}, f32[512,1024]{1,0:T(8,128)}, bf16[1024,512]{1,0:T(8,128)(2,1)}, bf16[16,64,16,128]{3,2,1,0:T(8,128)(2,1)}, bf16[...) custom-call(bf16[1024,1024]{1,0:T(8,128)(2,1)} %get-tuple-element.39.h2, ...), custom_call_target="tpu_custom_call" | custom-call | tf_op jit(solution)/shard_map/middle/pallas_call | solution.py:602
  116.0 134.1 %backward.1 = (bf16[4,128,1024]{2,1,0:T(8,128)(2,1)}, bf16[4,128,1024]{2,1,0:T(8,128)(2,1)}, f32[8,3072]{1,0:T(8,128)}, f32[8,1024]{1,0:T(8,128)}, f32[8,4096]{1...) custom-call(bf16[1024,1536]{1,0:T(8,128)(2,1)} %get-tuple-element.38.qkv, bf16[1024,512]{1,0:T(8,128)(2,1)} %get-tuple-element.43.dctx, ...), custom_call_target="tpu_custom_call" | custom-call | tf_op jit(solution)/shard_map/backward/pallas_call | solution.py:939
  250.2 0.0 copy-start.2
  250.2 0.0 copy-start.3
  250.2 0.0 copy-start.1
  250.2 0.0 copy-start
  250.2 0.9 copy.30
  251.1 0.6 fusion
  251.8 0.6 dynamic_slice.26
  252.3 0.6 dynamic_slice.30
  252.9 2.3 copy.45
  255.2 2.3 copy.46
  257.4 0.0 copy-done.2
  257.4 0.6 copy.47
  258.1 0.0 copy-done.3
  258.1 0.6 copy.48
  258.7 0.0 copy-done.1
  258.7 0.7 copy.49
  259.4 0.0 copy-done
  259.4 0.7 copy.50
  (1 shorter events, 0.0 us)
Async XLA Ops:
  250.2 7.3 %copy-start.2 = (f32[8,3072]{1,0:T(8,128)S(1)}, f32[8,3072]{1,0:T(8,128)}, u32[]{:S(2)}) copy-start(f32[8,3072]{1,0:T(8,128)} %get-tuple-element.86) | copy-start | bytes 294916
  250.2 7.9 %copy-start.3 = (f32[8,1024]{1,0:T(8,128)S(1)}, f32[8,1024]{1,0:T(8,128)}, u32[]{:S(2)}) copy-start(f32[8,1024]{1,0:T(8,128)} %get-tuple-element.88) | copy-start | bytes 98308
  250.2 8.5 %copy-start.1 = (f32[8,4096]{1,0:T(8,128)S(1)}, f32[8,4096]{1,0:T(8,128)}, u32[]{:S(2)}) copy-start(f32[8,4096]{1,0:T(8,128)} %get-tuple-element.92) | copy-start | bytes 393220
  250.2 9.2 %copy-start = (f32[32,1024]{1,0:T(8,128)S(1)}, f32[32,1024]{1,0:T(8,128)}, u32[]{:S(2)}) copy-start(f32[32,1024]{1,0:T(8,128)} %get-tuple-element.94) | copy-start | bytes 393220

commit v2 on v1

v2 whole, which is shorter than its diff:
```python
import jax
import jax.numpy as jnp
from jax import lax
from jax.experimental import pallas as pl
from jax.experimental.pallas import tpu as pltpu
from jax.sharding import Mesh, PartitionSpec as P

BF = jnp.bfloat16
F32 = jnp.float32
AXES = ("xh", "y", "c", "xl", "z")
BY_MESH = pl.DeviceIdType.MESH
DIMS = ("x1", "y1", "z1", "x0", "y0", "z0")
UP_ORDERS = (("y1", "y0", "x1", "z", "x0"), ("x1", "y0", "y1", "z", "x0"))
DOWN_GROUPS = (
    (0, 3, ("z1", "z0", "x0"), ("y", "x1")),
    (3, 6, ("z0", "x0", "z1"), ("y", "x1")),
    (6, 8, ("x0", "z1", "z0"), ("x1", "y")),
)
OUT_ORDERS = (("y", "x", "z"), ("x", "y", "z"), ("y", "z", "x"), ("y", "x", "z"))
QKV_ORDERS = (("x", "y", "z"), ("z", "x", "y"), ("y", "z", "x"))
BLOCK = 256
GELU = 0.7978845608028654
CUBIC = 0.044715
EPS = 1e-05
MASKED = -1e30
VMEM_LIMIT = 60 * 1024 * 1024


def dot_nn(a, b):
    return lax.dot_general(a, b, (((1,), (0,)), ((), ())), preferred_element_type=F32)


def dot_nt(a, b):
    return lax.dot_general(a, b, (((1,), (1,)), ((), ())), preferred_element_type=F32)


def dot_tn(a, b):
    return lax.dot_general(a, b, (((0,), (0,)), ((), ())), preferred_element_type=F32)


class Place:
    def __init__(self):
        self.xh, self.y, self.c, self.xl, self.z = (lax.axis_index(a) for a in AXES)
        two = jnp.int32(2)
        self.bits = {
            "x1": self.xh,
            "x0": lax.rem(self.xl + self.xh, two),
            "y1": lax.div(self.y, two),
            "y0": lax.rem(self.y + lax.div(self.y, two), two),
            "z1": lax.div(self.z, two),
            "z0": lax.rem(self.z + lax.div(self.z, two), two),
            "x": 2 * self.xh + self.xl,
            "y": self.y,
            "z": self.z,
        }

    def partner(self, name):
        xh, y, c, xl, z = self.xh, self.y, self.c, self.xl, self.z
        if name == "c":
            c = 1 - c
        elif name == "x0":
            xl = 1 - xl
        elif name == "x1":
            xh, xl = 1 - xh, 1 - xl
        elif name == "y0":
            y = y + 1 - 2 * lax.rem(y, jnp.int32(2))
        elif name == "y1":
            y = 3 - y
        elif name == "z0":
            z = z + 1 - 2 * lax.rem(z, jnp.int32(2))
        elif name == "z1":
            z = 3 - z
        return (xh, y, c, xl, z)

    def ring(self, axis, step):
        four, two = jnp.int32(4), jnp.int32(2)
        xh, y, c, xl, z = self.xh, self.y, self.c, self.xl, self.z
        if axis == "x":
            at = lax.rem(2 * xh + xl + step, four)
            xh, xl = lax.div(at, two), lax.rem(at, two)
        elif axis == "y":
            y = lax.rem(y + step, four)
        else:
            z = lax.rem(z + step, four)
        return (xh, y, c, xl, z)

    def exchange(self, r):
        return (self.xh, self.y, self.xl, self.c, jnp.int32(r))

    def is_self(self, r):
        return (self.c == self.xl) & (self.z == r)


def bits_of(s):
    xh, y, xl, z = s >> 5, (s >> 3) & 3, (s >> 2) & 1, s & 3
    return {
        "x1": xh, "y1": y >> 1, "z1": z >> 1, "x0": xl ^ xh, "y0": (y & 1) ^ (y >> 1), "z0": (z & 1) ^ (z >> 1),
        "x": 2 * xh + xl, "y": y, "z": z,
    }


def width(name):
    return 4 if len(name) == 1 else 2


def left_after(order, k):
    n = 1
    for name in order[k:]:
        n *= width(name)
    return n


def slot_of(s, order):
    bits, slot = bits_of(s), 0
    for name in order:
        slot = width(name) * slot + bits[name]
    return slot


def offset_before(place, order, k):
    off = jnp.int32(0)
    for j, name in enumerate(order[: k - 1]):
        off = off + place.bits[name] * left_after(order, j + 1)
    return off


def region(order, k):
    return sum((width(name) - 1) * left_after(order, j + 1) for j, name in enumerate(order[: k - 1]))


class Scatter:
    def __init__(self, place, k, order, buf, got, lead, sends, recvs, at):
        name = order[k - 1]
        n = left_after(order, k)
        first = offset_before(place, order, k)
        self.copies = []
        for s in range(1, width(name)):
            if width(name) == 2:
                peer, to = place.partner(name), 1 - place.bits[name]
            else:
                peer, to = place.ring(name, s), lax.rem(place.bits[name] + s, jnp.int32(4))
            self.copies.append(
                pltpu.make_async_remote_copy(
                    src_ref=buf.at[lead + (pl.ds(first + to * n, n),)],
                    dst_ref=got.at[lead + (pl.ds(region(order, k) + (s - 1) * n, n),)],
                    send_sem=sends.at[at + (s - 1,)],
                    recv_sem=recvs.at[at + (s - 1,)],
                    device_id=peer,
                    device_id_type=BY_MESH,
                )
            )

    def start(self):
        for copy in self.copies:
            copy.start()

    def wait(self):
        for copy in self.copies:
            copy.wait()


def scatter_sum(place, k, order, buf, got, lead):
    n = left_after(order, k)
    mine = lead + (pl.ds(offset_before(place, order, k + 1), n),)
    total = buf[mine].astype(F32)
    for s in range(1, width(order[k - 1])):
        total = total + got[lead + (pl.ds(region(order, k) + (s - 1) * n, n),)].astype(F32)
    return mine, total


def scatter_add(place, k, order, buf, got, lead):
    mine, total = scatter_sum(place, k, order, buf, got, lead)
    buf[mine] = total.astype(BF)


def scatter_last(place, order, buf, got, lead):
    _, total = scatter_sum(place, len(order), order, buf, got, lead)
    return total.reshape(total.shape[-2:])


def feature_rows(flat):
    parts = []
    for g in range(8):
        for c in range(2):
            parts.append(flat[(c * 8 + g) * 8 : (c * 8 + g + 1) * 8])
    return jnp.concatenate(parts, axis=0)


def transpose_features(src, dst):
    def body(f, carry):
        block = src[:, pl.ds(pl.multiple_of(f * 128, 128), 128)].astype(F32)
        dst[pl.ds(pl.multiple_of(f * 128, 128), 128), :] = feature_rows(block.T).astype(BF)
        return carry

    lax.fori_loop(0, 8, body, 0)


def norm_parts(v):
    center = v - jnp.mean(v, axis=-1, keepdims=True)
    rstd = lax.rsqrt(jnp.mean(center * center, axis=-1, keepdims=True) + EPS)
    return center * rstd, rstd


def aligned(v, m):
    return pl.multiple_of(v, m)


def window(i):
    return max(0, i - 2) * BLOCK, (i + 1) * BLOCK


def remote(src, dst, send, recv, device):
    return pltpu.make_async_remote_copy(
        src_ref=src, dst_ref=dst, send_sem=send, recv_sem=recv, device_id=device, device_id_type=BY_MESH
    )


def greet(place, devices, with_exchange):
    barrier = pltpu.get_barrier_semaphore()
    count = jnp.int32(len(devices))
    for d in devices:
        pl.semaphore_signal(barrier, inc=1, device_id=d, device_id_type=BY_MESH)
    if with_exchange:
        for r in range(4):

            @pl.when(jnp.logical_not(place.is_self(r)))
            def _(r=r):
                pl.semaphore_signal(barrier, inc=1, device_id=place.exchange(r), device_id_type=BY_MESH)

        count = count + 4 - jnp.where(place.c == place.xl, 1, 0)
    pl.semaphore_wait(barrier, count)


def exchange_start(place, src_of, dst_of, own_dst_of, sends, recvs):
    for r in range(4):
        own = place.is_self(r)

        @pl.when(own)
        def _(r=r):
            pltpu.make_async_copy(src_of(r), own_dst_of(r), recvs.at[place.z]).start()

        @pl.when(jnp.logical_not(own))
        def _(r=r):
            remote(src_of(r), dst_of(r), sends.at[r], recvs.at[place.z], place.exchange(r)).start()


def exchange_sent(place, src_of, dst_of, sends, recvs):
    for r in range(4):

        @pl.when(jnp.logical_not(place.is_self(r)))
        def _(r=r):
            remote(src_of(r), dst_of(r), sends.at[r], recvs.at[place.z], place.exchange(r)).wait_send()


def vmem(n=None):
    return pl.BlockSpec(memory_space=pltpu.VMEM)


def anywhere():
    return pl.BlockSpec(memory_space=pl.ANY)


def dma(*shape):
    return pltpu.SemaphoreType.DMA(shape)


def shaped(shape, dtype):
    return jax.ShapeDtypeStruct(shape, dtype)


def first_kernel(
    x_in, c_in, seg_in, flag_in, g1, b1_, bqv, bo, g2, b2_, bd, bu, wqkv, wout, wup, wdown,
    h1_o, qkv_o, x_o, ctxh_o, dres_o, dctx_o, lout_o, upleft_o, downleft_o, bout_o, lse_o, seg_o, par, small_o,
    hid, cot, qkv, x_own, ctxh, ctxp, resid, h2t, lse_acc, wq, wo, wu, wd, down_acc, dh_acc, act_s, dup_s, dat, lout, dctx,
    bup, rup, bdown, rdown, bout, upleft, downleft, seg_got,
    xs, xr, cs, cr, hs, hr, fs, fr, ts, tr, gs, gr, ss, sr, ws, us, ds, es, er, ups, upr, dns, dnr, os,
):
    place = Place()
    c, xl, z = place.c, place.xl, place.z
    mate = place.partner("c")
    own = pl.ds(aligned(c * 512, 512), 512)
    far = pl.ds(aligned((1 - c) * 512, 512), 512)
    loads = [
        pltpu.make_async_copy(
            wqkv.at[:, pl.ds(aligned(j * 1024 + c * 512, 512), 512)], wq.at[:, pl.ds(j * 512, 512)], ws.at[j]
        )
        for j in range(3)
    ]
    loads.append(pltpu.make_async_copy(wout, wo, ws.at[3]))

    def up_load(t):
        return pltpu.make_async_copy(
            wup.at[:, pl.ds(aligned((2 * t + c) * 256, 256), 256)], wu.at[lax.rem(t, jnp.int32(4))], us.at[t]
        )

    def down_load(t):
        return pltpu.make_async_copy(
            wdown.at[pl.ds(aligned((2 * t + c) * 256, 256), 256)], wd.at[lax.rem(t, jnp.int32(4))], ds.at[t]
        )

    def saves(n, src, dst):
        return pltpu.make_async_copy(src, dst, os.at[n])

    for load in loads:
        load.start()
    for t in range(4):
        up_load(jnp.int32(t)).start()
        down_load(jnp.int32(t)).start()
    greet(place, [mate] + [place.partner(d) for d in DIMS], True)

    def x_src(r):
        return x_in.at[r]

    def x_dst(r):
        return x_own.at[pl.ds(aligned(z * 128, 128), 128)]

    def c_src(r):
        return c_in.at[r]

    def c_dst(r):
        return cot.at[pl.ds(aligned(xl * 512 + z * 128, 128), 128)]

    exchange_start(place, x_src, x_dst, x_dst, xs, xr)
    seg_out = [remote(ref, seg_got.at[n], ss.at[n], sr.at[n], mate) for n, ref in enumerate((seg_in, flag_in))]
    for copy in seg_out:
        copy.start()
    for n, ref in enumerate((g1, b1_, bqv, bqv, bo, g2, b2_, bd, bu, bu, bu, bu)):
        first = {3: 1024, 9: 1024, 10: 2048, 11: 3072}.get(n, 0)
        par[n : n + 1, :] = ref[first : first + 1024].astype(F32).reshape(1, 1024)
    par[12:16, :] = jnp.zeros((4, 1024), F32)

    for copy in seg_out:
        copy.wait()
    own_seg, own_flag = seg_in[pl.ds(z, 1), :], flag_in[pl.ds(z, 1), :]
    far_seg, far_flag = seg_got[0, pl.ds(z, 1), :], seg_got[1, pl.ds(z, 1), :]
    near = jnp.where(c == xl, 1, 0)
    seg_row = jnp.where(near == 1, own_seg, far_seg).astype(F32)
    flag_row = jnp.where(near == 1, own_flag, far_flag)
    key_row = jnp.where(flag_row == 0, seg_row, -1.0)
    seg_o[...] = jnp.concatenate([seg_row, key_row, jnp.zeros((6, 1024), F32)], axis=0)
    seg_col = jnp.broadcast_to(seg_row, (128, 1024)).T
    for i in range(4):
        w0, w1 = window(i)
        rows = lax.broadcasted_iota(jnp.int32, (BLOCK, w1 - w0), 0) + i * BLOCK
        cols = lax.broadcasted_iota(jnp.int32, (BLOCK, w1 - w0), 1) + w0
        same = seg_col[i * BLOCK : (i + 1) * BLOCK, 0:1] == key_row[:, w0:w1]
        dh_acc[i * BLOCK : (i + 1) * BLOCK, 0 : w1 - w0] = jnp.where(
            (same & (cols <= rows)) | (rows == cols), 0.0, MASKED
        )
    lse_acc[...] = jnp.zeros_like(lse_acc)

    gain_one, bias_one = par[0:1, :], par[1:2, :]

    def block_copy(ref, b, mine, sends, recvs):
        half = c if mine else 1 - c
        rows = pl.ds(aligned(half * 512 + b * 128, 128), 128)
        return remote(ref.at[rows], ref.at[rows], sends.at[b], recvs.at[b], mate)

    for b in range(4):
        pltpu.make_async_copy(x_in.at[0], x_own.at[b * 128 : (b + 1) * 128], xr.at[b]).wait()
        xhat, _ = norm_parts(x_own[b * 128 : (b + 1) * 128].astype(F32))
        hid[pl.ds(aligned(c * 512 + b * 128, 128), 128)] = (xhat * gain_one + bias_one).astype(BF)
        block_copy(hid, b, True, hs, hr).start()
    exchange_start(place, c_src, c_dst, c_dst, cs, cr)
    saves(0, x_own, x_o).start()

    for load in loads[:3]:
        load.wait()
    zero = jnp.zeros((1, 512), F32)
    bias = jnp.concatenate([par[2:3, own], zero, par[3:4, own]], axis=1)

    def project(first):
        def body(n, carry):
            rows = pl.ds(aligned(first + n * BLOCK, BLOCK), BLOCK)
            qkv[rows, :] = (dot_nn(hid[rows, :], wq[...]) + bias).astype(BF)
            return carry

        lax.fori_loop(0, 2, body, 0)

    project(c * 512)
    for b in range(4):
        block_copy(hid, b, False, hs, hr).wait_recv()
    saves(1, hid, h1_o).start()
    project((1 - c) * 512)
    saves(2, qkv, qkv_o).start()

    lane = lax.broadcasted_iota(jnp.int32, (BLOCK, 128), 1)

    def ctx_copy(p, half):
        return remote(
            ctxh.at[far, pl.ds(aligned(p * 128, 128), 128)],
            ctxp.at[:, pl.ds(aligned(half * 512 + p * 128, 128), 128)],
            ts.at[p], tr.at[p], mate,
        )

    def attend(p, carry):
        lo = aligned(p * 128, 128)
        for i in range(4):
            w0, w1 = window(i)
            rows = slice(i * BLOCK, (i + 1) * BLOCK)
            query = qkv[rows, pl.ds(lo, 128)] * jnp.asarray(0.125, BF)
            keys = qkv[w0:w1, pl.ds(aligned(512 + lo, 128), 128)]
            values = qkv[w0:w1, pl.ds(aligned(1024 + lo, 128), 128)]
            outs = []
            lses = lse_acc[rows, :]
            for h in range(2):
                mine = (lane < 64) if h == 0 else (lane >= 64)
                scores = dot_nt(jnp.where(mine, query, jnp.zeros_like(query)), keys) + dh_acc[rows, 0 : w1 - w0]
                top = jnp.max(scores, axis=-1, keepdims=True)
                expo = jnp.exp(scores - top)
                total = jnp.sum(expo, axis=-1, keepdims=True)
                outs.append(dot_nn(expo.astype(BF), values) * (1.0 / total))
                lses = jnp.where(lane == 2 * p + h, top + jnp.log(total), lses)
            lse_acc[rows, :] = lses
            ctxh[rows, pl.ds(lo, 128)] = jnp.where(lane < 64, outs[0], outs[1]).astype(BF)

        @pl.when(p == 3)
        def _():
            saves(1, hid, h1_o).wait()
            saves(2, qkv, qkv_o).wait()
            for b in range(4):
                block_copy(hid, b, True, hs, hr).wait_send()

        ctx_copy(p, c).start()
        ctxp[:, pl.ds(aligned(c * 512 + lo, 128), 128)] = ctxh[own, pl.ds(lo, 128)]
        return carry

    lax.fori_loop(0, 4, attend, 0)
    saves(3, ctxh, ctxh_o).start()
    lse_o[...] = lse_acc[...].T[0:16, :]

    for b in range(4):
        pltpu.make_async_copy(c_in.at[0], cot.at[pl.ds(aligned(c * 512 + b * 128, 128), 128)], cr.at[b]).wait()
        block_copy(cot, b, True, fs, fr).start()

    loads[3].wait()
    for p in range(4):
        ctx_copy(p, 1 - c).wait_recv()

    def h2_copy(n, half):
        rows = pl.ds(aligned(half * 512 + n * BLOCK, BLOCK), BLOCK)
        return remote(hid.at[rows], hid.at[rows], gs.at[n], gr.at[n], mate)

    def output(n, carry):
        rows = pl.ds(aligned(n * BLOCK, BLOCK), BLOCK)
        res = x_own[rows, :].astype(F32) + (dot_nn(ctxp[rows, :], wo[...]) + par[4:5, :])
        resid[rows, :] = res
        xhat, _ = norm_parts(res)
        hid[pl.ds(aligned(c * 512 + n * BLOCK, BLOCK), BLOCK), :] = (xhat * par[5:6, :] + par[6:7, :]).astype(BF)
        h2_copy(n, c).start()
        return carry

    lax.fori_loop(0, 2, output, 0)
    small_o[...] = jnp.zeros_like(small_o)
    for n in range(2):
        h2_copy(n, 1 - c).wait_recv()
    transpose_features(hid, h2t)
    for b in range(4):
        block_copy(cot, b, False, fs, fr).wait_recv()

    def up_copy(k, t, j):
        return Scatter(place, k, UP_ORDERS[j], bup, rup, (t, j), ups, upr, (k - 1, t, j))

    def down_copy(k, t, g):
        p0, p1, order, _ = DOWN_GROUPS[g]
        return Scatter(place, k, order, bdown, rdown, (t, slice(p0, p1)), dns, dnr, (k - 1, t, g))

    def start(k, t):
        for j in range(2):
            up_copy(k, t, j).start()
        for g in range(3):
            down_copy(k, t, g).start()

    def tile_slot(t, rest):
        bits = {"x1": lax.div(t, jnp.int32(4)), "y": lax.rem(t, jnp.int32(4))}
        slot = jnp.int32(0)
        for name in rest:
            slot = width(name) * slot + bits[name]
        return slot

    def finish(k, t):
        for j in range(2):
            up_copy(k, t, j).wait()
        for g in range(3):
            down_copy(k, t, g).wait()
        for j, order in enumerate(UP_ORDERS):
            mine, total = scatter_sum(place, k, order, bup, rup, (t, j))
            if k < 3:
                bup[mine] = total.astype(BF)
            else:
                upleft[j, t] = total.astype(BF)
        for p0, p1, order, rest in DOWN_GROUPS:
            for p in range(p0, p1):
                mine, total = scatter_sum(place, k, order, bdown, rdown, (t, p))
                if k < 3:
                    bdown[mine] = total.astype(BF)
                else:
                    downleft[p, pl.ds(tile_slot(t, rest), 1)] = total.astype(BF)
        if k < 3:
            start(k + 1, t)

    def tile(t, carry):
        four = jnp.int32(4)
        ring = lax.rem(t, four)
        up_load(t).wait()
        down_load(t).wait()
        col = 2 * t + c
        up_row = 8 + lax.div(col, four)
        up_cols = pl.ds(aligned(lax.rem(col, four) * 256, 256), 256)
        up_bias = par[pl.ds(up_row, 1), up_cols]
        dbias = jnp.zeros((1, 256), F32)
        for b in range(4):
            rows = slice(b * BLOCK, (b + 1) * BLOCK)
            u = dot_nn(hid[rows, :], wu[ring]) + up_bias
            dact = dot_nt(cot[rows, :], wd[ring])
            square = u * u
            th = jnp.tanh(GELU * u * (1.0 + CUBIC * square))
            act_s[rows, :] = (0.5 * u * (1.0 + th)).astype(BF)
            slope = 0.5 * (1.0 + th) + 0.5 * u * (1.0 - th * th) * (GELU * (1.0 + (3.0 * CUBIC) * square))
            dup = (dact * slope).astype(BF)
            dup_s[rows, :] = dup
            dbias = dbias + jnp.sum(dup.astype(F32), axis=0, keepdims=True)
        small_o[pl.ds(up_row, 1), up_cols] = dbias

        for k in (3, 2, 1):

            @pl.when(t >= k + 1)
            def _(k=k):
                finish(k, t - k - 1)

        xh = lax.div(t, four)
        grad = dot_tn(act_s[...], cot[...]).astype(BF)
        for s in range(8):
            bits = bits_of(s)
            x0 = lax.rem(xh + (s >> 2), jnp.int32(2))
            for p0, p1, order, _ in DOWN_GROUPS:
                fixed = sum(bits[name] << (2 - n) for n, name in enumerate(order) if name != "x0")
                slot = fixed + x0 * (1 << (2 - order.index("x0")))
                for j in range(p0, p1):
                    bdown[t, j, slot] = grad[s * 32 : (s + 1) * 32, j * 128 : (j + 1) * 128]
        for b in range(4):
            grad = dot_nn(h2t[b * 256 : (b + 1) * 256, :], dup_s[...]).astype(BF)
            for s in range(16):
                for j, order in enumerate(UP_ORDERS):
                    bup[t, j, slot_of(b * 16 + s, order)] = grad[s * 16 : (s + 1) * 16, j * 128 : (j + 1) * 128]
        start(1, t)

        @pl.when(t == 0)
        def _():
            for b in range(4):
                rows = slice(b * BLOCK, (b + 1) * BLOCK)
                down_acc[rows, :] = dot_nn(act_s[rows, :], wd[ring])
                dh_acc[rows, :] = dot_nt(dup_s[rows, :], wu[ring])

        @pl.when(t > 0)
        def _():
            for b in range(4):
                rows = slice(b * BLOCK, (b + 1) * BLOCK)
                down_acc[rows, :] = down_acc[rows, :] + dot_nn(act_s[rows, :], wd[ring])
                dh_acc[rows, :] = dh_acc[rows, :] + dot_nt(dup_s[rows, :], wu[ring])

        @pl.when(t < 4)
        def _():
            up_load(t + 4).start()
            down_load(t + 4).start()

        return carry

    lax.fori_loop(0, 8, tile, 0)

    dh_send, dh_got = qkv.at[0:512, 0:1024], qkv.at[512:1024, 0:1024]
    dn_send, dn_got = wq.at[0:512, 0:1024], wq.at[512:1024, 0:1024]
    dc_send = qkv.at[0:512, 1024:1536]
    ctxt = wq.at[:, 1024:1536]
    wo_send, wo_got = bup.at[0:2], bup.at[2:4]
    dh_send[...] = dh_acc[far, :].astype(BF)
    dh_copy = remote(dh_send, dh_got, es.at[0], er.at[0], mate)
    dh_copy.start()
    dn_send[...] = down_acc[far, :].astype(BF)
    dn_copy = remote(dn_send, dn_got, es.at[1], er.at[1], mate)
    dn_copy.start()
    for k in (3, 2, 1):
        finish(k, 7 - k)

    transpose_features(ctxp, ctxt)
    dh_copy.wait()
    dn_copy.wait()

    def norm_back(n, sums):
        gain_sum, bias_sum, out_sum, down_sum = sums
        rows = pl.ds(aligned(n * 128, 128), 128)
        mine = pl.ds(aligned(c * 512 + n * 128, 128), 128)
        res = resid[rows, :]
        lout[rows, :] = (res + (down_acc[mine, :] + dn_got[rows, :].astype(F32) + par[7:8, :])).astype(BF)
        xhat, rstd = norm_parts(res)
        dn = dh_acc[mine, :] + dh_got[rows, :].astype(F32)
        e = dn * par[5:6, :]
        cf = cot[mine, :].astype(F32)
        dres = cf + rstd * (
            e - jnp.mean(e, axis=-1, keepdims=True) - xhat * jnp.mean(e * xhat, axis=-1, keepdims=True)
        )
        resid[rows, :] = dres
        low = dres.astype(BF)
        dat[rows, :] = low
        return (
            gain_sum + jnp.sum(dn * xhat, axis=0, keepdims=True),
            bias_sum + jnp.sum(dn, axis=0, keepdims=True),
            out_sum + jnp.sum(low.astype(F32), axis=0, keepdims=True),
            down_sum + jnp.sum(cf, axis=0, keepdims=True),
        )

    nothing = jnp.zeros((1, 1024), F32)
    gain_sum, bias_sum, out_sum, down_sum = lax.fori_loop(0, 4, norm_back, (nothing,) * 4)
    small_o[5:6, :] = gain_sum
    small_o[6:7, :] = bias_sum
    small_o[4:5, :] = out_sum
    small_o[7:8, :] = down_sum
    saves(4, resid, dres_o).start()
    saves(5, lout, lout_o).start()

    dc_send[...] = dot_nt(dat[...], wo[far, :]).astype(BF)
    dc_copy = remote(dc_send, dctx.at[own], es.at[2], er.at[2], mate)
    dc_copy.start()
    for k in (3, 2, 1):
        finish(k, 8 - k)

    def out_grad(cols, dst, lead):
        for b in range(4):
            grad = dot_nn(ctxt[b * 256 : (b + 1) * 256, :], dat[:, cols]).astype(BF)
            for s in range(16):
                for j, order in enumerate(OUT_ORDERS):
                    dst[lead(j) + (slot_of(b * 16 + s, order),)] = grad[s * 16 : (s + 1) * 16, j * 128 : (j + 1) * 128]

    out_grad(far, wo_send, lambda j: (j // 2, j % 2))
    wo_copy = remote(wo_send, wo_got, es.at[3], er.at[3], mate)
    wo_copy.start()
    dctx[own, :] = dot_nt(dat[...], wo[own, :]).astype(BF)
    for k in (3, 2):
        finish(k, 9 - k)
    out_grad(own, bout, lambda j: (j,))
    dc_copy.wait_send()
    remote(dc_send, dctx.at[far], es.at[2], er.at[2], mate).wait_recv()
    saves(6, dctx, dctx_o).start()
    finish(3, 7)
    saves(7, upleft, upleft_o).start()
    saves(8, downleft, downleft_o).start()
    wo_copy.wait()
    for j in range(4):
        bout[j] = bout[j] + wo_got[j // 2, j % 2]
    saves(9, bout, bout_o).start()

    exchange_sent(place, x_src, x_dst, xs, xr)
    exchange_sent(place, c_src, c_dst, cs, cr)
    for b in range(4):
        block_copy(cot, b, True, fs, fr).wait_send()
        ctx_copy(b, c).wait_send()
    for n in range(2):
        h2_copy(n, c).wait_send()
    saves(0, x_own, x_o).wait()
    saves(3, ctxh, ctxh_o).wait()
    saves(4, resid, dres_o).wait()
    saves(5, lout, lout_o).wait()
    saves(6, dctx, dctx_o).wait()
    saves(7, upleft, upleft_o).wait()
    saves(8, downleft, downleft_o).wait()
    saves(9, bout, bout_o).wait()


def run_first(*args):
    outs = (
        shaped((1024, 1024), BF), shaped((1024, 1536), BF), shaped((512, 1024), BF), shaped((1024, 512), BF),
        shaped((512, 1024), F32), shaped((1024, 512), BF), shaped((512, 1024), BF), shaped((2, 8, 8, 16, 128), BF),
        shaped((8, 8, 32, 128), BF), shaped((4, 64, 16, 128), BF), shaped((16, 1024), F32), shaped((8, 1024), F32),
        shaped((16, 1024), F32), shaped((16, 1024), F32),
    )
    v = pltpu.VMEM
    return pl.pallas_call(
        first_kernel,
        out_shape=outs,
        in_specs=[anywhere(), anywhere()] + [vmem()] * 10 + [anywhere()] * 4,
        out_specs=(anywhere(),) * 10 + (vmem(),) * 4,
        scratch_shapes=[
            v((1024, 1024), BF), v((1024, 1024), BF), v((1024, 1536), BF), v((512, 1024), BF), v((1024, 512), BF),
            v((512, 1024), BF), v((512, 1024), F32), v((1024, 1024), BF), v((1024, 128), F32), v((1024, 1536), BF),
            v((1024, 1024), BF), v((4, 1024, 256), BF), v((4, 256, 1024), BF), v((1024, 1024), F32),
            v((1024, 1024), F32), v((1024, 256), BF), v((1024, 256), BF), v((512, 1024), BF), v((512, 1024), BF),
            v((1024, 512), BF), v((8, 2, 64, 16, 128), BF), v((8, 2, 56, 16, 128), BF), v((8, 8, 8, 32, 128), BF),
            v((8, 8, 7, 32, 128), BF), v((4, 64, 16, 128), BF), v((2, 8, 8, 16, 128), BF), v((8, 8, 32, 128), BF),
            v((2, 4, 1024), jnp.int32),
            dma(4), dma(4), dma(4), dma(4), dma(4), dma(4), dma(4), dma(4), dma(4), dma(4), dma(2), dma(2), dma(2),
            dma(2), dma(4), dma(8), dma(8), dma(4), dma(4), dma(3, 8, 2, 1), dma(3, 8, 2, 1), dma(3, 8, 3, 1),
            dma(3, 8, 3, 1), dma(10),
        ],
        compiler_params=pltpu.CompilerParams(collective_id=0, has_side_effects=True, vmem_limit_bytes=VMEM_LIMIT),
        name="first",
    )(*args)


MAIN = (
    tuple((0, (j, slice(0, 8)), UP_ORDERS[j][3:]) for j in range(2))
    + tuple((1, (slice(p0, p1),), rest) for p0, p1, _, rest in DOWN_GROUPS)
    + tuple((2, (j,), order) for j, order in enumerate(OUT_ORDERS))
)
EVENTS = {(0, 3): 1, (1, 3): 2, (2, 3): 3}


def backward_kernel(
    qkv, dctx, ctxh, lse, seg, h1, x_own, dres, small_in, par, lout, upleft, downleft, bout_in, wqkv,
    lout_o, gin_o, gqkv_o, gout_o, gup_o, gdown_o, small_o,
    wq, h1t, dqkv, dk_acc, dv_acc, drow, t0, t1, t2, t3, bup, bdown, bout, bqkv, rup, rdown, rout, rqkv,
    fin_up, fin_out, fin_qkv, far_up, far_out, far_qkv, dh_send, dh_got, dh_own, gin_s,
    sm, sm_first, sm_acc, sm_got, sm_last,
    ws, ms, mr, qs, qr, ls, lr, gs, gr, hs, hr, es, er, ps, pr,
):
    place = Place()
    c, xl, z = place.c, place.xl, place.z
    mate = place.partner("c")
    loads = [
        pltpu.make_async_copy(upleft, bup, ws.at[0]),
        pltpu.make_async_copy(downleft, bdown, ws.at[1]),
        pltpu.make_async_copy(bout_in, bout, ws.at[2]),
    ]
    for p in range(4):
        for j in range(3):
            loads.append(
                pltpu.make_async_copy(
                    wqkv.at[:, pl.ds(aligned(j * 1024 + c * 512 + p * 128, 128), 128)],
                    wq.at[:, pl.ds(p * 384 + j * 128, 128)],
                    ws.at[3 + p * 3 + j],
                )
            )
    for load in loads:
        load.start()
    peers = [mate] + [place.partner(d) for d in DIMS] + [place.ring(a, s) for a in "xyz" for s in (1, 2, 3)]
    greet(place, peers, True)

    def l_src(r):
        return lout.at[pl.ds(r * 128, 128)]

    def l_dst(r):
        return lout_o.at[z]

    exchange_start(place, l_src, l_dst, l_dst, ls, lr)
    for load in loads[:3]:
        load.wait()
    bufs, gots = (bup, bdown, bout), (rup, rdown, rout)

    def steps(k):
        return [n for n, (_, _, order) in enumerate(MAIN) if k <= len(order)]

    def main_copy(k, n):
        which, lead, order = MAIN[n]
        return Scatter(place, k, order, bufs[which], gots[which], lead, ms, mr, (k - 1, n))

    def main_start(k):
        for n in steps(k):
            main_copy(k, n).start()

    def main_finish(k):
        for n in steps(k):
            main_copy(k, n).wait()
        for n in steps(k):
            which, lead, order = MAIN[n]
            if k < len(order):
                scatter_add(place, k, order, bufs[which], gots[which], lead)
        if k < 3:
            main_start(k + 1)
        if k == 2:
            left_last()
        if k == 3:
            out_last()

    main_start(1)

    key_col = jnp.broadcast_to(seg[1:2, :], (128, 1024)).T
    for i, ref in enumerate((t0, t1, t2, t3)):
        w0, w1 = window(i)
        rows = lax.broadcasted_iota(jnp.int32, (w1 - w0, BLOCK), 0) + w0
        cols = lax.broadcasted_iota(jnp.int32, (w1 - w0, BLOCK), 1) + i * BLOCK
        same = key_col[w0:w1, 0:1] == seg[0:1, i * BLOCK : (i + 1) * BLOCK]
        ref[...] = jnp.where((same & (rows <= cols)) | (rows == cols), 0.0, MASKED)
    transpose_features(h1, h1t)
    sm[...] = small_in[...]

    lane = lax.broadcasted_iota(jnp.int32, (BLOCK, 128), 1)
    head_of = lax.broadcasted_iota(jnp.int32, (16, 128), 1)
    row_of = lax.broadcasted_iota(jnp.int32, (16, 128), 0)
    pick = jnp.where(lax.div(head_of, jnp.int32(64)) == row_of, 1.0, 0.0).astype(BF)

    def far_copy(src, dst, at):
        return remote(src.at[pl.ds(aligned((1 - c) * 8, 8), 8)], dst, es.at[at], er.at[at], mate)

    def left_last():
        for j in range(2):
            for t in range(8):
                p = 2 * t + j
                fin_up[:, p * 128 : (p + 1) * 128] = scatter_last(place, UP_ORDERS[j][3:], bup, rup, (j, t))
        far_copy(fin_up, far_up, 0).start()
        for p0, p1, _, rest in DOWN_GROUPS:
            for p in range(p0, p1):
                gdown_o[:, p * 128 : (p + 1) * 128] = scatter_last(place, rest, bdown, rdown, (p,))

    def out_last():
        for j, order in enumerate(OUT_ORDERS):
            fin_out[:, j * 128 : (j + 1) * 128] = scatter_last(place, order, bout, rout, (j,))
        far_copy(fin_out, far_out, 1).start()

    def qkv_copy(k, p, j):
        return Scatter(place, k, QKV_ORDERS[j], bqkv, rqkv, (p, j), qs, qr, (k - 1, p, j))

    def qkv_start(k, p):
        for j in range(3):
            qkv_copy(k, p, j).start()

    def qkv_finish(k, p):
        for j in range(3):
            qkv_copy(k, p, j).wait()
        for j, order in enumerate(QKV_ORDERS):
            if k < 3:
                scatter_add(place, k, order, bqkv, rqkv, (p, j))
            else:
                fin_qkv[:, pl.ds(aligned(j * 512 + p * 128, 128), 128)] = scatter_last(place, order, bqkv, rqkv, (p, j))
        if k < 3:
            qkv_start(k + 1, p)

    def pair(p, carry):
        lo = aligned(p * 128, 128)
        prod = (dctx[:, pl.ds(lo, 128)].astype(F32) * ctxh[:, pl.ds(lo, 128)].astype(F32)).astype(BF)
        drow[...] = dot_nt(pick, prod)
        dk_acc[...] = jnp.zeros_like(dk_acc)
        dv_acc[...] = jnp.zeros_like(dv_acc)
        at = p * 384
        for i, ref in enumerate((t0, t1, t2, t3)):
            w0, w1 = window(i)
            rows = slice(i * BLOCK, (i + 1) * BLOCK)
            query = qkv[rows, pl.ds(lo, 128)] * jnp.asarray(0.125, BF)
            keys = qkv[w0:w1, pl.ds(aligned(512 + lo, 128), 128)]
            values = qkv[w0:w1, pl.ds(aligned(1024 + lo, 128), 128)]
            grad = dctx[rows, pl.ds(lo, 128)]
            dq = []
            for h in range(2):
                mine = (lane < 64) if h == 0 else (lane >= 64)
                query_h = jnp.where(mine, query, jnp.zeros_like(query))
                grad_h = jnp.where(mine, grad, jnp.zeros_like(grad))
                scores = dot_nt(keys, query_h) + ref[...]
                probs = jnp.exp(scores - lse[pl.ds(2 * p + h, 1), rows])
                dprobs = dot_nt(values, grad_h)
                dscores = (probs * (dprobs - drow[h : h + 1, rows])).astype(BF)
                dv_acc[w0:w1, :] = dv_acc[w0:w1, :] + dot_nn(probs.astype(BF), grad_h)
                dk_acc[w0:w1, :] = dk_acc[w0:w1, :] + dot_nn(dscores, query_h)
                dq.append(dot_tn(dscores, keys))
            dqkv[rows, pl.ds(aligned(at, 128), 128)] = (jnp.where(lane < 64, dq[0], dq[1]) * 0.125).astype(BF)
            for (ep, ei), k in EVENTS.items():
                if ei == i:

                    @pl.when(p == ep)
                    def _(k=k):
                        main_finish(k)

            if i == 2:
                for back in (3, 2):

                    @pl.when(p >= back)
                    def _(back=back):
                        qkv_finish(back - 1, p - back)

        dqkv[:, pl.ds(aligned(at + 128, 128), 128)] = dk_acc[...].astype(BF)
        dqkv[:, pl.ds(aligned(at + 256, 128), 128)] = dv_acc[...].astype(BF)
        own = pl.ds(aligned(c * 512 + lo, 128), 128)
        sm[2:3, own] = jnp.sum(dqkv[:, pl.ds(aligned(at, 128), 128)].astype(F32), axis=0, keepdims=True)
        sm[3:4, own] = jnp.sum(dqkv[:, pl.ds(aligned(at + 256, 128), 128)].astype(F32), axis=0, keepdims=True)
        for b in range(4):
            grad = dot_nn(h1t[b * 256 : (b + 1) * 256, :], dqkv[:, pl.ds(aligned(at, 128), 384)]).astype(BF)
            for s in range(16):
                for j, order in enumerate(QKV_ORDERS):
                    bqkv[p, j, slot_of(b * 16 + s, order)] = grad[s * 16 : (s + 1) * 16, j * 128 : (j + 1) * 128]
        qkv_start(1, p)
        return carry

    lax.fori_loop(0, 4, pair, 0)

    def tail(n):
        for k in (3, 2, 1):
            p = n + 2 - k
            if p < 4 and (k, p) not in ((2, 0), (1, 1), (1, 0)):
                qkv_finish(k, p)

    for load in loads[3:]:
        load.wait()

    def dh_copy(n):
        rows = pl.ds(aligned(n * BLOCK, BLOCK), BLOCK)
        return remote(dh_send.at[rows], dh_got.at[rows], hs.at[n], hr.at[n], mate)

    def far_half(n, carry):
        rows = pl.ds(aligned((1 - c) * 512 + n * BLOCK, BLOCK), BLOCK)
        dh_send[pl.ds(aligned(n * BLOCK, BLOCK), BLOCK), :] = dot_nt(dqkv[rows, :], wq[...]).astype(BF)
        dh_copy(n).start()
        return carry

    lax.fori_loop(0, 2, far_half, 0)
    tail(1)

    def own_half(n, carry):
        rows = pl.ds(aligned(c * 512 + n * BLOCK, BLOCK), BLOCK)
        dh_own[pl.ds(aligned(n * BLOCK, BLOCK), BLOCK), :] = dot_nt(dqkv[rows, :], wq[...])
        return carry

    lax.fori_loop(0, 2, own_half, 0)
    tail(2)
    for n in range(2):
        dh_copy(n).wait()

    def norm_back(n, sums):
        gain_sum, bias_sum = sums
        rows = pl.ds(aligned(n * 128, 128), 128)
        xhat, rstd = norm_parts(x_own[rows, :].astype(F32))
        dn = dh_own[rows, :] + dh_got[rows, :].astype(F32)
        e = dn * par[0:1, :]
        gin_s[rows, :] = (
            dres[rows, :]
            + rstd * (e - jnp.mean(e, axis=-1, keepdims=True) - xhat * jnp.mean(e * xhat, axis=-1, keepdims=True))
        ).astype(BF)
        return (
            gain_sum + jnp.sum(dn * xhat, axis=0, keepdims=True),
            bias_sum + jnp.sum(dn, axis=0, keepdims=True),
        )

    nothing = jnp.zeros((1, 1024), F32)
    gain_sum, bias_sum = lax.fori_loop(0, 4, norm_back, (nothing,) * 2)
    sm[0:1, :] = gain_sum
    sm[1:2, :] = bias_sum

    own8 = pl.ds(aligned(c * 8, 8), 8)
    far8 = pl.ds(aligned((1 - c) * 8, 8), 8)
    small_copy = remote(sm.at[far8], sm_first, es.at[3], er.at[3], mate)
    small_copy.start()

    def g_src(r):
        return gin_s.at[pl.ds(r * 128, 128)]

    def g_dst(r):
        return gin_o.at[z]

    exchange_start(place, g_src, g_dst, g_dst, gs, gr)
    tail(3)

    small_copy.wait()
    sm_acc[0] = sm[own8, :] + sm_first[...]

    def phase_copy(n, s):
        return remote(sm_acc.at[n], sm_got.at[n, s - 1], ps.at[n, s - 1], pr.at[n, s - 1], place.ring("zyx"[n], s))

    for n in range(3):
        for s in (1, 2, 3):
            phase_copy(n, s).start()
        if n < 2:
            tail(4 + n)
        if n == 1:
            far_copy(fin_qkv, far_qkv, 4).start()
        for s in (1, 2, 3):
            phase_copy(n, s).wait()
        sm_acc[n + 1] = sm_acc[n] + sm_got[n, 0] + sm_got[n, 1] + sm_got[n, 2]

    last_copy = remote(sm_acc.at[3], sm_last, es.at[5], er.at[5], mate)
    last_copy.start()

    own8 = pl.ds(aligned(c * 8, 8), 8)
    far_copy(fin_up, far_up, 0).wait()
    for t in range(8):
        mine, theirs = fin_up[own8, t * 256 : (t + 1) * 256], far_up[:, t * 256 : (t + 1) * 256]
        gup_o[:, t * 512 : t * 512 + 256] = jnp.where(c == 0, mine, theirs)
        gup_o[:, t * 512 + 256 : t * 512 + 512] = jnp.where(c == 0, theirs, mine)
    far_copy(fin_out, far_out, 1).wait()
    mine, theirs = fin_out[own8, :], far_out[...]
    gout_o[:, 0:512] = jnp.where(c == 0, mine, theirs)
    gout_o[:, 512:1024] = jnp.where(c == 0, theirs, mine)
    far_copy(fin_qkv, far_qkv, 4).wait()
    for j in range(3):
        mine, theirs = fin_qkv[own8, j * 512 : (j + 1) * 512], far_qkv[:, j * 512 : (j + 1) * 512]
        gqkv_o[:, j * 1024 : j * 1024 + 512] = jnp.where(c == 0, mine, theirs)
        gqkv_o[:, j * 1024 + 512 : j * 1024 + 1024] = jnp.where(c == 0, theirs, mine)
    last_copy.wait()
    mine, theirs = sm_acc[3], sm_last[...]
    small_o[0:8, :] = jnp.where(c == 0, mine, theirs)
    small_o[8:16, :] = jnp.where(c == 0, theirs, mine)

    exchange_sent(place, l_src, l_dst, ls, lr)
    exchange_sent(place, g_src, g_dst, gs, gr)
    for b in range(4):
        pltpu.make_async_copy(lout.at[pl.ds(0, 128)], lout_o.at[b], lr.at[b]).wait()
        pltpu.make_async_copy(gin_s.at[pl.ds(0, 128)], gin_o.at[b], gr.at[b]).wait()


def run_backward(*args):
    outs = (
        shaped((4, 128, 1024), BF), shaped((4, 128, 1024), BF), shaped((8, 3072), F32), shaped((8, 1024), F32),
        shaped((8, 4096), F32), shaped((32, 1024), F32), shaped((16, 1024), F32),
    )
    v = pltpu.VMEM
    return pl.pallas_call(
        backward_kernel,
        out_shape=outs,
        in_specs=[vmem()] * 10 + [anywhere()] * 5,
        out_specs=(anywhere(), anywhere()) + (vmem(),) * 5,
        scratch_shapes=[
            v((1024, 1536), BF), v((1024, 1024), BF), v((1024, 1536), BF), v((1024, 128), F32), v((1024, 128), F32),
            v((16, 1024), F32), v((256, 256), F32), v((512, 256), F32), v((768, 256), F32), v((768, 256), F32),
            v((2, 8, 8, 16, 128), BF), v((8, 8, 32, 128), BF), v((4, 64, 16, 128), BF), v((4, 3, 64, 16, 128), BF),
            v((2, 8, 7, 16, 128), BF), v((8, 7, 32, 128), BF), v((4, 63, 16, 128), BF), v((4, 3, 63, 16, 128), BF),
            v((16, 2048), F32), v((16, 512), F32), v((16, 1536), F32), v((8, 2048), F32), v((8, 512), F32),
            v((8, 1536), F32), v((512, 1024), BF), v((512, 1024), BF), v((512, 1024), F32), v((512, 1024), BF),
            v((16, 1024), F32), v((8, 1024), F32), v((4, 8, 1024), F32), v((3, 3, 8, 1024), F32), v((8, 1024), F32),
            dma(15), dma(3, 9, 3), dma(3, 9, 3), dma(3, 4, 3, 3), dma(3, 4, 3, 3), dma(4), dma(4), dma(4), dma(4), dma(2), dma(2),
            dma(6), dma(6), dma(3, 3), dma(3, 3),
        ],
        compiler_params=pltpu.CompilerParams(collective_id=1, has_side_effects=True, vmem_limit_bytes=VMEM_LIMIT),
        name="backward",
    )(*args)


VECTORS = ((0, 8), (1, 8), (2, 16), (4, 8), (5, 8), (6, 8), (8, 32), (7, 8))


def finish_kernel(*refs):
    lout, gin, gqkv, gout, gup, gdown, sums = refs[:7]
    outs, vectors = refs[7:13], refs[13:21]
    for src, dst in zip((lout, gin, gqkv, gout, gup, gdown), outs):
        dst[...] = src[...]
    place = Place()
    device = ((place.xh * 4 + place.y) * 2 + place.c) * 8 + place.xl * 4 + place.z
    for (row, size), out in zip(VECTORS, vectors):
        first = device * size
        line = row + lax.div(first, jnp.int32(1024))
        turned = pltpu.roll(sums[pl.ds(line, 1), :], 1024 - lax.rem(first, jnp.int32(1024)), 1)
        out[...] = turned[0, :size]


def run_finish(*args):
    outs = tuple(shaped(a.shape, a.dtype) for a in args[:6]) + tuple(shaped((size,), F32) for _, size in VECTORS)
    return pl.pallas_call(
        finish_kernel,
        out_shape=outs,
        in_specs=[vmem()] * 7,
        out_specs=(vmem(),) * 14,
        name="finish",
    )(*args)


def on_device(
    block_input, segment_ids, padding_flags, cotangent, norm_one_gain, norm_one_bias, query_key_value, query_value_bias,
    out_weight, out_bias, norm_two_gain, norm_two_bias, up_weight, up_bias, down_weight, down_bias,
):
    h1, qkv, x_own, ctxh, dres, dctx, lout, upleft, downleft, bout, lse, seg, par, small = run_first(
        block_input, cotangent, segment_ids, padding_flags, norm_one_gain, norm_one_bias, query_value_bias, out_bias,
        norm_two_gain, norm_two_bias, down_bias, up_bias, query_key_value, out_weight, up_weight, down_weight,
    )
    results = run_backward(
        qkv, dctx, ctxh, lse, seg, h1, x_own, dres, small, par, lout, upleft, downleft, bout, query_key_value
    )
    lout, gin, gqkv, gout, gup, gdown, n1g, n1b, qvb, ob, n2g, n2b, ub, db = run_finish(*results)
    return (lout, gin, n1g, n1b, gqkv, qvb, gout, ob, n2g, n2b, gup, ub, gdown, db)


def solution(mesh):
    wide = Mesh(mesh.devices.reshape(2, 4, 2, 2, 4), AXES)
    rows, seq = ("xh", "y", "c"), ("xl", "z")
    everything = rows + seq
    whole = P()
    return jax.shard_map(
        on_device,
        mesh=wide,
        in_specs=(P(rows, seq, None), P(rows, None), P(rows, None), P(rows, seq, None)) + (whole,) * 12,
        out_specs=(
            P(rows, seq, None), P(rows, seq, None), P(everything), P(everything), P(everything, None), P(everything),
            P(everything, None), P(everything), P(everything), P(everything), P(everything, None), P(everything),
            P(everything, None), P(everything),
        ),
        check_vma=False,
    )
```

time: 261 us -> 202 us (0.77)
  Pallas kernels: 243 us -> 201 us
  local copies, waits for them, and re-layouts: 16 us -> 0 us
    pallas_call x1, Pallas kernels: 134 us -> 91.1 us  [run_backward(): pl.pallas_call(backward_kernel, out_shape=outs, in_specs=[vmem()] * 10 +...]
    unnamed x23 -> x0, local copies, waits for them, and re-layouts: 13.5 us -> none
where the time goes in v2:
time: 202 us
  Pallas kernels  201 us (100%)
    pallas_call x1, Pallas kernels, run_first(): pl.pallas_call(first_kernel, out_shape=outs, in_specs=[anywhere(), anywhe...  107 us
    pallas_call x1, Pallas kernels, run_backward(): pl.pallas_call(backward_kernel, out_shape=outs, in_specs=[vmem()] * 10 +...  91.1 us

profile of v2, /device:TPU:1, one launch (start us, length us, event | category | flops | bytes accessed | tf_op | source)
XLA Modules:
  0.0 201.8 jit_solution(17375488622132724121)
XLA Ops:
  0.7 106.6 %first.1 = (bf16[1024,1024]{1,0:T(8,128)(2,1)}, bf16[1024,1536]{1,0:T(8,128)(2,1)}, bf16[512,1024]{1,0:T(8,128)(2,1)}, bf16[1024,512]{1,0:T(8,128)(2,1)}, f32[51...) custom-call(bf16[4,128,1024]{2,1,0:T(8,128)(2,1)} %x_in.1, ...), custom_call_target="tpu_custom_call" | custom-call | tf_op jit(solution)/shard_map/first/pallas_call | solution.py:677
  107.3 91.1 %backward.1 = (bf16[4,128,1024]{2,1,0:T(8,128)(2,1)}, bf16[4,128,1024]{2,1,0:T(8,128)(2,1)}, f32[8,3072]{1,0:T(8,128)}, f32[8,1024]{1,0:T(8,128)}, f32[8,4096]{1...) custom-call(bf16[1024,1536]{1,0:T(8,128)(2,1)} %get-tuple-element.49.qkv, bf16[1024,512]{1,0:T(8,128)(2,1)} %get-tuple-element.50.dctx, ...), custom_call_target="tpu_custom_call" | custom-call | tf_op jit(solution)/shard_map/backward/pallas_call | solution.py:1001
  198.4 3.3 %finish.1 = (bf16[4,128,1024]{2,1,0:T(8,128)(2,1)}, bf16[4,128,1024]{2,1,0:T(8,128)(2,1)}, f32[8,3072]{1,0:T(8,128)}, f32[8,1024]{1,0:T(8,128)}, f32[8,4096]{1,0...) custom-call(bf16[4,128,1024]{2,1,0:T(8,128)(2,1)} %get-tuple-element, ...), custom_call_target="tpu_custom_call" | custom-call | tf_op jit(solution)/shard_map/finish/pallas_call | solution.py:1041

commit v3 on v2

--- a/solution.py
+++ b/solution.py
@@ -10,13 +10,13 @@
 AXES = ("xh", "y", "c", "xl", "z")
 BY_MESH = pl.DeviceIdType.MESH
 DIMS = ("x1", "y1", "z1", "x0", "y0", "z0")
-UP_ORDERS = (("y1", "y0", "x1", "z", "x0"), ("x1", "y0", "y1", "z", "x0"))
+UP_ORDERS = (("y1", "y0", "x1", "z", "x0"), ("x1", "y0", "y1", "x0", "z"))
 DOWN_GROUPS = (
     (0, 3, ("z1", "z0", "x0"), ("y", "x1")),
-    (3, 6, ("z0", "x0", "z1"), ("y", "x1")),
+    (3, 6, ("z0", "x0", "z1"), ("x1", "y")),
     (6, 8, ("x0", "z1", "z0"), ("x1", "y")),
 )
-OUT_ORDERS = (("y", "x", "z"), ("x", "y", "z"), ("y", "z", "x"), ("y", "x", "z"))
+OUT_ORDERS = (("y", "x", "z"), ("y", "z", "x"), ("y", "x", "z"), ("y", "z", "x"))
 QKV_ORDERS = (("x", "y", "z"), ("z", "x", "y"), ("y", "z", "x"))
 BLOCK = 256
 GELU = 0.7978845608028654
@@ -53,8 +53,29 @@
             "y": self.y,
             "z": self.z,
         }
+        names = ("c", "x1", "y1", "z1", "x0", "y0", "z0")
+        self.partners = {name: self.find_partner(name) for name in names}
+        self.rings = {(axis, s): self.find_ring(axis, s) for axis in "xyz" for s in (1, 2, 3)}
+        self.send, self.keep = {}, {}
+
+    def prepare(self, orders):
+        for order in orders:
+            off = jnp.int32(0)
+            for k, name in enumerate(order, 1):
+                n = left_after(order, k)
+                for s in range(1, width(name)):
+                    to = 1 - self.bits[name] if width(name) == 2 else lax.rem(self.bits[name] + s, jnp.int32(4))
+                    self.send[order, k, s] = off + to * n
+                off = off + self.bits[name] * n
+                self.keep[order, k] = off
 
     def partner(self, name):
+        return self.partners[name]
+
+    def ring(self, axis, step):
+        return self.rings[axis, step]
+
+    def find_partner(self, name):
         xh, y, c, xl, z = self.xh, self.y, self.c, self.xl, self.z
         if name == "c":
             c = 1 - c
@@ -72,7 +93,7 @@
             z = 3 - z
         return (xh, y, c, xl, z)
 
-    def ring(self, axis, step):
+    def find_ring(self, axis, step):
         four, two = jnp.int32(4), jnp.int32(2)
         xh, y, c, xl, z = self.xh, self.y, self.c, self.xl, self.z
         if axis == "x":
@@ -117,13 +138,6 @@
     return slot
 
 
-def offset_before(place, order, k):
-    off = jnp.int32(0)
-    for j, name in enumerate(order[: k - 1]):
-        off = off + place.bits[name] * left_after(order, j + 1)
-    return off
-
-
 def region(order, k):
     return sum((width(name) - 1) * left_after(order, j + 1) for j, name in enumerate(order[: k - 1]))
 
@@ -132,16 +146,12 @@
     def __init__(self, place, k, order, buf, got, lead, sends, recvs, at):
         name = order[k - 1]
         n = left_after(order, k)
-        first = offset_before(place, order, k)
         self.copies = []
         for s in range(1, width(name)):
-            if width(name) == 2:
-                peer, to = place.partner(name), 1 - place.bits[name]
-            else:
-                peer, to = place.ring(name, s), lax.rem(place.bits[name] + s, jnp.int32(4))
+            peer = place.partner(name) if width(name) == 2 else place.ring(name, s)
             self.copies.append(
                 pltpu.make_async_remote_copy(
-                    src_ref=buf.at[lead + (pl.ds(first + to * n, n),)],
+                    src_ref=buf.at[lead + (pl.ds(place.send[order, k, s], n),)],
                     dst_ref=got.at[lead + (pl.ds(region(order, k) + (s - 1) * n, n),)],
                     send_sem=sends.at[at + (s - 1,)],
                     recv_sem=recvs.at[at + (s - 1,)],
@@ -161,7 +171,9 @@
 
 def scatter_sum(place, k, order, buf, got, lead):
     n = left_after(order, k)
-    mine = lead + (pl.ds(offset_before(place, order, k + 1), n),)
+    mine = lead + (pl.ds(place.keep[order, k], n),)
+    if width(order[k - 1]) == 2 and k < len(order):
+        return mine, buf[mine] + got[lead + (pl.ds(region(order, k), n),)]
     total = buf[mine].astype(F32)
     for s in range(1, width(order[k - 1])):
         total = total + got[lead + (pl.ds(region(order, k) + (s - 1) * n, n),)].astype(F32)
@@ -186,10 +198,14 @@
     return jnp.concatenate(parts, axis=0)
 
 
-def transpose_features(src, dst):
+def natural_rows(flat):
+    return jnp.concatenate([flat[(g * 2 + c) * 8 : (g * 2 + c + 1) * 8] for c in range(2) for g in range(8)], axis=0)
+
+
+def transpose_features(src, dst, tokens):
     def body(f, carry):
-        block = src[:, pl.ds(pl.multiple_of(f * 128, 128), 128)].astype(F32)
-        dst[pl.ds(pl.multiple_of(f * 128, 128), 128), :] = feature_rows(block.T).astype(BF)
+        block = src[tokens, pl.ds(pl.multiple_of(f * 128, 128), 128)].astype(F32)
+        dst[pl.ds(pl.multiple_of(f * 128, 128), 128), tokens] = feature_rows(block.T).astype(BF)
         return carry
 
     lax.fori_loop(0, 8, body, 0)
@@ -231,8 +247,8 @@
     pl.semaphore_wait(barrier, count)
 
 
-def exchange_start(place, src_of, dst_of, own_dst_of, sends, recvs):
-    for r in range(4):
+def exchange_start(place, src_of, dst_of, own_dst_of, sends, recvs, which=(0, 1, 2, 3)):
+    for r in which:
         own = place.is_self(r)
 
         @pl.when(own)
@@ -278,6 +294,7 @@
     place = Place()
     c, xl, z = place.c, place.xl, place.z
     mate = place.partner("c")
+    place.prepare(UP_ORDERS + tuple(g[2] for g in DOWN_GROUPS))
     own = pl.ds(aligned(c * 512, 512), 512)
     far = pl.ds(aligned((1 - c) * 512, 512), 512)
     loads = [
@@ -401,18 +418,20 @@
             query = qkv[rows, pl.ds(lo, 128)] * jnp.asarray(0.125, BF)
             keys = qkv[w0:w1, pl.ds(aligned(512 + lo, 128), 128)]
             values = qkv[w0:w1, pl.ds(aligned(1024 + lo, 128), 128)]
-            outs = []
-            lses = lse_acc[rows, :]
-            for h in range(2):
-                mine = (lane < 64) if h == 0 else (lane >= 64)
-                scores = dot_nt(jnp.where(mine, query, jnp.zeros_like(query)), keys) + dh_acc[rows, 0 : w1 - w0]
-                top = jnp.max(scores, axis=-1, keepdims=True)
-                expo = jnp.exp(scores - top)
-                total = jnp.sum(expo, axis=-1, keepdims=True)
-                outs.append(dot_nn(expo.astype(BF), values) * (1.0 / total))
-                lses = jnp.where(lane == 2 * p + h, top + jnp.log(total), lses)
-            lse_acc[rows, :] = lses
-            ctxh[rows, pl.ds(lo, 128)] = jnp.where(lane < 64, outs[0], outs[1]).astype(BF)
+            zero = jnp.zeros_like(query)
+            both = jnp.concatenate([jnp.where(lane < 64, query, zero), jnp.where(lane < 64, zero, query)], axis=0)
+            mask = dh_acc[rows, 0 : w1 - w0]
+            scores = dot_nt(both, keys) + jnp.concatenate([mask, mask], axis=0)
+            top = jnp.max(scores, axis=-1, keepdims=True)
+            expo = jnp.exp(scores - top)
+            found = dot_nn(expo.astype(BF), jnp.concatenate([values, jnp.ones_like(values)], axis=1))
+            total = found[:, 128:256]
+            log_total = top + jnp.log(total)
+            outs = found[:, 0:128] / total
+            lse_acc[rows, :] = jnp.where(
+                lane == 2 * p, log_total[:BLOCK], jnp.where(lane == 2 * p + 1, log_total[BLOCK:], lse_acc[rows, :])
+            )
+            ctxh[rows, pl.ds(lo, 128)] = jnp.where(lane < 64, outs[:BLOCK], outs[BLOCK:]).astype(BF)
 
         @pl.when(p == 3)
         def _():
@@ -452,9 +471,10 @@
 
     lax.fori_loop(0, 2, output, 0)
     small_o[...] = jnp.zeros_like(small_o)
+    transpose_features(hid, h2t, own)
     for n in range(2):
         h2_copy(n, 1 - c).wait_recv()
-    transpose_features(hid, h2t)
+    transpose_features(hid, h2t, far)
     for b in range(4):
         block_copy(cot, b, False, fs, fr).wait_recv()
 
@@ -582,7 +602,7 @@
     for k in (3, 2, 1):
         finish(k, 7 - k)
 
-    transpose_features(ctxp, ctxt)
+    transpose_features(ctxp, ctxt, slice(0, 512))
     dh_copy.wait()
     dn_copy.wait()
 
@@ -701,32 +721,42 @@
     + tuple((1, (slice(p0, p1),), rest) for p0, p1, _, rest in DOWN_GROUPS)
     + tuple((2, (j,), order) for j, order in enumerate(OUT_ORDERS))
 )
-EVENTS = {(0, 3): 1, (1, 3): 2, (2, 3): 3}
+LEFT = (0, 1, 2, 3, 4)
+OUT = (5, 6, 7, 8)
+EVENTS = {
+    (0, 3): (("left", 1), ("early", 0)),
+    (1, 3): (("left", 2), ("early", 1)),
+    (2, 1): (("out", 1),),
+    (2, 3): (("early", 2),),
+    (3, 1): (("out", 2),),
+}
 
 
 def backward_kernel(
-    qkv, dctx, ctxh, lse, seg, h1, x_own, dres, small_in, par, lout, upleft, downleft, bout_in, wqkv,
+    lse, seg, small_in, par, upleft, downleft, bout_in, qkv_in, dctx_in, ctxh_in, h1_in, lout_in, wqkv, x_in, dres_in,
     lout_o, gin_o, gqkv_o, gout_o, gup_o, gdown_o, small_o,
+    qkv, dctx, ctxh, h1, lout, x_own, dres,
     wq, h1t, dqkv, dk_acc, dv_acc, drow, t0, t1, t2, t3, bup, bdown, bout, bqkv, rup, rdown, rout, rqkv,
-    fin_up, fin_out, fin_qkv, far_up, far_out, far_qkv, dh_send, dh_got, dh_own, gin_s,
-    sm, sm_first, sm_acc, sm_got, sm_last,
-    ws, ms, mr, qs, qr, ls, lr, gs, gr, hs, hr, es, er, ps, pr,
+    fin_up, fin_out, fin_qkv, far_up, far_out, far_qkv, dh_send, dh_got, dh_acc, gin_s, gain_acc, bias_acc,
+    early, early_got, early_far, late, late_got, late_far,
+    ws, ms, mr, qs, qr, ls, lr, gs, gr, hs, hr, es, er, ps, pr, vs, vr,
 ):
     place = Place()
     c, xl, z = place.c, place.xl, place.z
     mate = place.partner("c")
-    loads = [
-        pltpu.make_async_copy(upleft, bup, ws.at[0]),
-        pltpu.make_async_copy(downleft, bdown, ws.at[1]),
-        pltpu.make_async_copy(bout_in, bout, ws.at[2]),
-    ]
+    place.prepare(tuple(order for _, _, order in MAIN) + QKV_ORDERS)
+    moves = (
+        (upleft, bup), (downleft, bdown), (bout_in, bout), (qkv_in, qkv), (dctx_in, dctx), (ctxh_in, ctxh), (h1_in, h1),
+        (lout_in, lout), (x_in, x_own), (dres_in, dres),
+    )
+    loads = [pltpu.make_async_copy(src, dst, ws.at[n]) for n, (src, dst) in enumerate(moves)]
     for p in range(4):
         for j in range(3):
             loads.append(
                 pltpu.make_async_copy(
                     wqkv.at[:, pl.ds(aligned(j * 1024 + c * 512 + p * 128, 128), 128)],
                     wq.at[:, pl.ds(p * 384 + j * 128, 128)],
-                    ws.at[3 + p * 3 + j],
+                    ws.at[10 + p * 3 + j],
                 )
             )
     for load in loads:
@@ -740,37 +770,66 @@
     def l_dst(r):
         return lout_o.at[z]
 
-    exchange_start(place, l_src, l_dst, l_dst, ls, lr)
     for load in loads[:3]:
         load.wait()
     bufs, gots = (bup, bdown, bout), (rup, rdown, rout)
 
-    def steps(k):
-        return [n for n, (_, _, order) in enumerate(MAIN) if k <= len(order)]
-
     def main_copy(k, n):
         which, lead, order = MAIN[n]
         return Scatter(place, k, order, bufs[which], gots[which], lead, ms, mr, (k - 1, n))
 
-    def main_start(k):
-        for n in steps(k):
+    def main_start(k, which):
+        for n in which:
             main_copy(k, n).start()
 
-    def main_finish(k):
-        for n in steps(k):
+    def main_finish(k, which):
+        for n in which:
             main_copy(k, n).wait()
-        for n in steps(k):
-            which, lead, order = MAIN[n]
+        for n in which:
+            b, lead, order = MAIN[n]
             if k < len(order):
-                scatter_add(place, k, order, bufs[which], gots[which], lead)
-        if k < 3:
-            main_start(k + 1)
-        if k == 2:
+                scatter_add(place, k, order, bufs[b], gots[b], lead)
+        if k < len(MAIN[which[0]][2]):
+            main_start(k + 1, which)
+        elif which is LEFT:
             left_last()
-        if k == 3:
+        else:
             out_last()
 
-    main_start(1)
+    def vector_copy(ref, got, sends, recvs, n, s):
+        return remote(ref.at[n], got.at[n, s - 1], sends.at[n, s - 1], recvs.at[n, s - 1], place.ring("yxz"[n], s))
+
+    def vector_start(ref, got, sends, recvs, n):
+        for s in (1, 2, 3):
+            vector_copy(ref, got, sends, recvs, n, s).start()
+
+    def vector_finish(ref, got, sends, recvs, n):
+        for s in (1, 2, 3):
+            vector_copy(ref, got, sends, recvs, n, s).wait()
+        ref[n + 1] = ref[n] + got[n, 0] + got[n, 1] + got[n, 2]
+        if n < 2:
+            vector_start(ref, got, sends, recvs, n + 1)
+
+    early_copy = remote(early.at[3], early_far, es.at[3], er.at[3], mate)
+    late_copy = remote(late.at[3], late_far, es.at[5], er.at[5], mate)
+
+    def happen(what, k):
+        if what == "left":
+            main_finish(k, LEFT)
+        elif what == "out":
+            main_finish(k, OUT)
+        else:
+            vector_finish(early, early_got, ps, pr, k)
+            if k == 2:
+                early_copy.start()
+
+    main_start(1, LEFT)
+    early[0] = small_in[4:12, :]
+    vector_start(early, early_got, ps, pr, 0)
+    main_start(1, OUT)
+    loads[7].wait()
+    exchange_start(place, l_src, l_dst, l_dst, ls, lr)
+    late[0] = jnp.zeros((32, 128), F32)
 
     key_col = jnp.broadcast_to(seg[1:2, :], (128, 1024)).T
     for i, ref in enumerate((t0, t1, t2, t3)):
@@ -779,10 +838,14 @@
         cols = lax.broadcasted_iota(jnp.int32, (w1 - w0, BLOCK), 1) + i * BLOCK
         same = key_col[w0:w1, 0:1] == seg[0:1, i * BLOCK : (i + 1) * BLOCK]
         ref[...] = jnp.where((same & (rows <= cols)) | (rows == cols), 0.0, MASKED)
-    transpose_features(h1, h1t)
-    sm[...] = small_in[...]
+    for load in loads[3:7]:
+        load.wait()
+    transpose_features(h1, h1t, slice(0, 1024))
+    gain_acc[...] = jnp.zeros_like(gain_acc)
+    bias_acc[...] = jnp.zeros_like(bias_acc)
 
     lane = lax.broadcasted_iota(jnp.int32, (BLOCK, 128), 1)
+    row = lax.broadcasted_iota(jnp.int32, (128, BLOCK), 0)
     head_of = lax.broadcasted_iota(jnp.int32, (16, 128), 1)
     row_of = lax.broadcasted_iota(jnp.int32, (16, 128), 0)
     pick = jnp.where(lax.div(head_of, jnp.int32(64)) == row_of, 1.0, 0.0).astype(BF)
@@ -837,25 +900,26 @@
             keys = qkv[w0:w1, pl.ds(aligned(512 + lo, 128), 128)]
             values = qkv[w0:w1, pl.ds(aligned(1024 + lo, 128), 128)]
             grad = dctx[rows, pl.ds(lo, 128)]
-            dq = []
-            for h in range(2):
-                mine = (lane < 64) if h == 0 else (lane >= 64)
-                query_h = jnp.where(mine, query, jnp.zeros_like(query))
-                grad_h = jnp.where(mine, grad, jnp.zeros_like(grad))
-                scores = dot_nt(keys, query_h) + ref[...]
-                probs = jnp.exp(scores - lse[pl.ds(2 * p + h, 1), rows])
-                dprobs = dot_nt(values, grad_h)
-                dscores = (probs * (dprobs - drow[h : h + 1, rows])).astype(BF)
-                dv_acc[w0:w1, :] = dv_acc[w0:w1, :] + dot_nn(probs.astype(BF), grad_h)
-                dk_acc[w0:w1, :] = dk_acc[w0:w1, :] + dot_nn(dscores, query_h)
-                dq.append(dot_tn(dscores, keys))
-            dqkv[rows, pl.ds(aligned(at, 128), 128)] = (jnp.where(lane < 64, dq[0], dq[1]) * 0.125).astype(BF)
-            for (ep, ei), k in EVENTS.items():
+            zero = jnp.zeros_like(query)
+            both = jnp.concatenate([jnp.where(lane < 64, query, zero), jnp.where(lane < 64, zero, query)], axis=0)
+            grads = jnp.concatenate([jnp.where(lane < 64, grad, zero), jnp.where(lane < 64, zero, grad)], axis=0)
+            mask = ref[...]
+            log_total = jnp.concatenate([lse[pl.ds(2 * p, 1), rows], lse[pl.ds(2 * p + 1, 1), rows]], axis=1)
+            inner = jnp.concatenate([drow[0:1, rows], drow[1:2, rows]], axis=1)
+            probs = jnp.exp(dot_nt(keys, both) + jnp.concatenate([mask, mask], axis=1) - log_total)
+            dscores = (probs * (dot_nt(values, grads) - inner)).astype(BF)
+            dv_acc[w0:w1, :] = dv_acc[w0:w1, :] + dot_nn(probs.astype(BF), grads)
+            dk_acc[w0:w1, :] = dk_acc[w0:w1, :] + dot_nn(dscores, both)
+            dq = dot_tn(keys, dscores)
+            dq = jnp.where(row < 64, dq[:, :BLOCK], dq[:, BLOCK:]).T
+            dqkv[rows, pl.ds(aligned(at, 128), 128)] = (dq * 0.125).astype(BF)
+            for (ep, ei), events in EVENTS.items():
                 if ei == i:
 
                     @pl.when(p == ep)
-                    def _(k=k):
-                        main_finish(k)
+                    def _(events=events):
+                        for event in events:
+                            happen(*event)
 
             if i == 2:
                 for back in (3, 2):
@@ -866,14 +930,35 @@
 
         dqkv[:, pl.ds(aligned(at + 128, 128), 128)] = dk_acc[...].astype(BF)
         dqkv[:, pl.ds(aligned(at + 256, 128), 128)] = dv_acc[...].astype(BF)
-        own = pl.ds(aligned(c * 512 + lo, 128), 128)
-        sm[2:3, own] = jnp.sum(dqkv[:, pl.ds(aligned(at, 128), 128)].astype(F32), axis=0, keepdims=True)
-        sm[3:4, own] = jnp.sum(dqkv[:, pl.ds(aligned(at + 256, 128), 128)].astype(F32), axis=0, keepdims=True)
+        cols = pl.ds(aligned(at, 128), 384)
+        sums = jnp.sum(dqkv[:, cols].astype(F32), axis=0, keepdims=True)
+        late[0, pl.ds(16 + c * 4 + p, 1), :] = sums[:, 0:128]
+        late[0, pl.ds(24 + c * 4 + p, 1), :] = sums[:, 256:384]
+
+        @pl.when(p == 0)
+        def _():
+            for load in loads[10:]:
+                load.wait()
+
         for b in range(4):
-            grad = dot_nn(h1t[b * 256 : (b + 1) * 256, :], dqkv[:, pl.ds(aligned(at, 128), 384)]).astype(BF)
+            block = slice(b * 256, (b + 1) * 256)
+            grad = dot_nn(h1t[block, :], dqkv[:, cols])
+            low = grad.astype(BF)
             for s in range(16):
                 for j, order in enumerate(QKV_ORDERS):
-                    bqkv[p, j, slot_of(b * 16 + s, order)] = grad[s * 16 : (s + 1) * 16, j * 128 : (j + 1) * 128]
+                    bqkv[p, j, slot_of(b * 16 + s, order)] = low[s * 16 : (s + 1) * 16, j * 128 : (j + 1) * 128]
+            weight = wq[block, cols].astype(F32)
+            weight = jnp.concatenate([feature_rows(weight[0:128]), feature_rows(weight[128:256])], axis=0)
+            by_gain, by_bias = grad * weight, weight * sums
+            gain_acc[block, :] = gain_acc[block, :] + by_gain[:, 0:128] + by_gain[:, 128:256] + by_gain[:, 256:384]
+            bias_acc[block, :] = bias_acc[block, :] + by_bias[:, 0:128] + by_bias[:, 128:256] + by_bias[:, 256:384]
+
+        @pl.when(p == 1)
+        def _():
+            for b in range(4):
+                block = slice(b * 256, (b + 1) * 256)
+                dh_acc[block, :] = dot_nt(dqkv[block, 0:768], wq[:, 0:768])
+
         qkv_start(1, p)
         return carry
 
@@ -885,85 +970,59 @@
             if p < 4 and (k, p) not in ((2, 0), (1, 1), (1, 0)):
                 qkv_finish(k, p)
 
-    for load in loads[3:]:
-        load.wait()
+    def total_of(acc):
+        flat = jnp.concatenate([natural_rows(acc[g * 128 : (g + 1) * 128, :]) for g in range(8)], axis=0)
+        return jnp.sum(flat.T, axis=0, keepdims=True)
+
+    bias_sum = total_of(bias_acc)
+    gain_sum = (total_of(gain_acc) - par[1:2, :] * bias_sum) / par[0:1, :]
+    for l in range(8):
+        late[0, l : l + 1, :] = gain_sum[:, l * 128 : (l + 1) * 128]
+        late[0, 8 + l : 9 + l, :] = bias_sum[:, l * 128 : (l + 1) * 128]
+    vector_start(late, late_got, vs, vr, 0)
 
     def dh_copy(n):
         rows = pl.ds(aligned(n * BLOCK, BLOCK), BLOCK)
         return remote(dh_send.at[rows], dh_got.at[rows], hs.at[n], hr.at[n], mate)
 
-    def far_half(n, carry):
+    def second_half(rows):
+        return dh_acc[rows, :] + dot_nt(dqkv[rows, 768:1536], wq[:, 768:1536])
+
+    for n in range(2):
         rows = pl.ds(aligned((1 - c) * 512 + n * BLOCK, BLOCK), BLOCK)
-        dh_send[pl.ds(aligned(n * BLOCK, BLOCK), BLOCK), :] = dot_nt(dqkv[rows, :], wq[...]).astype(BF)
+        dh_send[n * BLOCK : (n + 1) * BLOCK, :] = second_half(rows).astype(BF)
         dh_copy(n).start()
-        return carry
-
-    lax.fori_loop(0, 2, far_half, 0)
     tail(1)
-
-    def own_half(n, carry):
-        rows = pl.ds(aligned(c * 512 + n * BLOCK, BLOCK), BLOCK)
-        dh_own[pl.ds(aligned(n * BLOCK, BLOCK), BLOCK), :] = dot_nt(dqkv[rows, :], wq[...])
-        return carry
-
-    lax.fori_loop(0, 2, own_half, 0)
-    tail(2)
+    for load in loads[8:10]:
+        load.wait()
+
+    def g_src(r):
+        return gin_s.at[pl.ds(r * 128, 128)]
+
+    def g_dst(r):
+        return gin_o.at[z]
+
     for n in range(2):
+        block = slice(n * BLOCK, (n + 1) * BLOCK)
+        dh = second_half(pl.ds(aligned(c * 512 + n * BLOCK, BLOCK), BLOCK))
         dh_copy(n).wait()
-
-    def norm_back(n, sums):
-        gain_sum, bias_sum = sums
-        rows = pl.ds(aligned(n * 128, 128), 128)
-        xhat, rstd = norm_parts(x_own[rows, :].astype(F32))
-        dn = dh_own[rows, :] + dh_got[rows, :].astype(F32)
-        e = dn * par[0:1, :]
-        gin_s[rows, :] = (
-            dres[rows, :]
+        xhat, rstd = norm_parts(x_own[block, :].astype(F32))
+        e = (dh + dh_got[block, :].astype(F32)) * par[0:1, :]
+        gin_s[block, :] = (
+            dres[block, :]
             + rstd * (e - jnp.mean(e, axis=-1, keepdims=True) - xhat * jnp.mean(e * xhat, axis=-1, keepdims=True))
         ).astype(BF)
-        return (
-            gain_sum + jnp.sum(dn * xhat, axis=0, keepdims=True),
-            bias_sum + jnp.sum(dn, axis=0, keepdims=True),
-        )
-
-    nothing = jnp.zeros((1, 1024), F32)
-    gain_sum, bias_sum = lax.fori_loop(0, 4, norm_back, (nothing,) * 2)
-    sm[0:1, :] = gain_sum
-    sm[1:2, :] = bias_sum
-
-    own8 = pl.ds(aligned(c * 8, 8), 8)
-    far8 = pl.ds(aligned((1 - c) * 8, 8), 8)
-    small_copy = remote(sm.at[far8], sm_first, es.at[3], er.at[3], mate)
-    small_copy.start()
-
-    def g_src(r):
-        return gin_s.at[pl.ds(r * 128, 128)]
-
-    def g_dst(r):
-        return gin_o.at[z]
-
-    exchange_start(place, g_src, g_dst, g_dst, gs, gr)
+        exchange_start(place, g_src, g_dst, g_dst, gs, gr, (2 * n, 2 * n + 1))
+        if n == 0:
+            vector_finish(late, late_got, vs, vr, 0)
+    tail(2)
+    main_finish(3, OUT)
+    vector_finish(late, late_got, vs, vr, 1)
     tail(3)
-
-    small_copy.wait()
-    sm_acc[0] = sm[own8, :] + sm_first[...]
-
-    def phase_copy(n, s):
-        return remote(sm_acc.at[n], sm_got.at[n, s - 1], ps.at[n, s - 1], pr.at[n, s - 1], place.ring("zyx"[n], s))
-
-    for n in range(3):
-        for s in (1, 2, 3):
-            phase_copy(n, s).start()
-        if n < 2:
-            tail(4 + n)
-        if n == 1:
-            far_copy(fin_qkv, far_qkv, 4).start()
-        for s in (1, 2, 3):
-            phase_copy(n, s).wait()
-        sm_acc[n + 1] = sm_acc[n] + sm_got[n, 0] + sm_got[n, 1] + sm_got[n, 2]
-
-    last_copy = remote(sm_acc.at[3], sm_last, es.at[5], er.at[5], mate)
-    last_copy.start()
+    vector_finish(late, late_got, vs, vr, 2)
+    late_copy.start()
+    tail(4)
+    far_copy(fin_qkv, far_qkv, 4).start()
 
     own8 = pl.ds(aligned(c * 8, 8), 8)
     far_copy(fin_up, far_up, 0).wait()
@@ -980,10 +1039,14 @@
         mine, theirs = fin_qkv[own8, j * 512 : (j + 1) * 512], far_qkv[:, j * 512 : (j + 1) * 512]
         gqkv_o[:, j * 1024 : j * 1024 + 512] = jnp.where(c == 0, mine, theirs)
         gqkv_o[:, j * 1024 + 512 : j * 1024 + 1024] = jnp.where(c == 0, theirs, mine)
-    last_copy.wait()
-    mine, theirs = sm_acc[3], sm_last[...]
-    small_o[0:8, :] = jnp.where(c == 0, mine, theirs)
-    small_o[8:16, :] = jnp.where(c == 0, theirs, mine)
+    early_copy.wait()
+    small_o[4:12, :] = early[3] + early_far[...]
+    small_o[12:16, :] = jnp.zeros((4, 1024), F32)
+    late_copy.wait()
+    total = late[3] + late_far[...]
+    for n in range(4):
+        for l in range(8):
+            small_o[n : n + 1, l * 128 : (l + 1) * 128] = total[n * 8 + l : n * 8 + l + 1, :]
 
     exchange_sent(place, l_src, l_dst, ls, lr)
     exchange_sent(place, g_src, g_dst, gs, gr)
@@ -1001,18 +1064,21 @@
     return pl.pallas_call(
         backward_kernel,
         out_shape=outs,
-        in_specs=[vmem()] * 10 + [anywhere()] * 5,
+        in_specs=[vmem()] * 4 + [anywhere()] * 11,
         out_specs=(anywhere(), anywhere()) + (vmem(),) * 5,
         scratch_shapes=[
+            v((1024, 1536), BF), v((1024, 512), BF), v((1024, 512), BF), v((1024, 1024), BF), v((512, 1024), BF),
+            v((512, 1024), BF), v((512, 1024), F32),
             v((1024, 1536), BF), v((1024, 1024), BF), v((1024, 1536), BF), v((1024, 128), F32), v((1024, 128), F32),
             v((16, 1024), F32), v((256, 256), F32), v((512, 256), F32), v((768, 256), F32), v((768, 256), F32),
             v((2, 8, 8, 16, 128), BF), v((8, 8, 32, 128), BF), v((4, 64, 16, 128), BF), v((4, 3, 64, 16, 128), BF),
             v((2, 8, 7, 16, 128), BF), v((8, 7, 32, 128), BF), v((4, 63, 16, 128), BF), v((4, 3, 63, 16, 128), BF),
             v((16, 2048), F32), v((16, 512), F32), v((16, 1536), F32), v((8, 2048), F32), v((8, 512), F32),
-            v((8, 1536), F32), v((512, 1024), BF), v((512, 1024), BF), v((512, 1024), F32), v((512, 1024), BF),
-            v((16, 1024), F32), v((8, 1024), F32), v((4, 8, 1024), F32), v((3, 3, 8, 1024), F32), v((8, 1024), F32),
-            dma(15), dma(3, 9, 3), dma(3, 9, 3), dma(3, 4, 3, 3), dma(3, 4, 3, 3), dma(4), dma(4), dma(4), dma(4), dma(2), dma(2),
-            dma(6), dma(6), dma(3, 3), dma(3, 3),
+            v((8, 1536), F32), v((512, 1024), BF), v((512, 1024), BF), v((1024, 1024), F32), v((512, 1024), BF),
+            v((1024, 128), F32), v((1024, 128), F32),
+            v((4, 8, 1024), F32), v((3, 3, 8, 1024), F32), v((8, 1024), F32), v((4, 32, 128), F32), v((3, 3, 32, 128), F32),
+            v((32, 128), F32), dma(22), dma(3, 9, 3), dma(3, 9, 3), dma(3, 4, 3, 3), dma(3, 4, 3, 3), dma(4), dma(4), dma(4), dma(4), dma(2), dma(2),
+            dma(6), dma(6), dma(3, 3), dma(3, 3), dma(3, 3), dma(3, 3),
         ],
         compiler_params=pltpu.CompilerParams(collective_id=1, has_side_effects=True, vmem_limit_bytes=VMEM_LIMIT),
         name="backward",
@@ -1056,7 +1122,7 @@
         norm_two_gain, norm_two_bias, down_bias, up_bias, query_key_value, out_weight, up_weight, down_weight,
     )
     results = run_backward(
-        qkv, dctx, ctxh, lse, seg, h1, x_own, dres, small, par, lout, upleft, downleft, bout, query_key_value
+        lse, seg, small, par, upleft, downleft, bout, qkv, dctx, ctxh, h1, lout, query_key_value, x_own, dres
     )
     lout, gin, gqkv, gout, gup, gdown, n1g, n1b, qvb, ob, n2g, n2b, ub, db = run_finish(*results)
     return (lout, gin, n1g, n1b, gqkv, qvb, gout, ob, n2g, n2b, gup, ub, gdown, db)

time: 202 us -> 184 us (0.911)
  Pallas kernels: 201 us -> 182 us
    pallas_call x1, Pallas kernels: 91.1 us -> 75.7 us  [run_backward(): pl.pallas_call(backward_kernel, out_shape=outs, in_specs=[vmem()] * 4 + [...]
    pallas_call x1, Pallas kernels: 107 us -> 103 us  [run_first(): pl.pallas_call(first_kernel, out_shape=outs, in_specs=[anywhere(), anywhe...]
where the time goes in v3:
time: 184 us; the launch traced here: 183 us
  Pallas kernels  182 us (99%)
    pallas_call x1, Pallas kernels, run_first(): pl.pallas_call(first_kernel, out_shape=outs, in_specs=[anywhere(), anywhe...  103 us
    pallas_call x1, Pallas kernels, run_backward(): pl.pallas_call(backward_kernel, out_shape=outs, in_specs=[vmem()] * 4 + [...  75.7 us

profile of v3, /device:TPU:1, one launch (start us, length us, event | category | flops | bytes accessed | tf_op | source)
XLA Modules:
  0.0 183.3 jit_solution(17307005313055117023)
XLA Ops:
  0.7 103.5 %first.1 = (bf16[1024,1024]{1,0:T(8,128)(2,1)}, bf16[1024,1536]{1,0:T(8,128)(2,1)}, bf16[512,1024]{1,0:T(8,128)(2,1)}, bf16[1024,512]{1,0:T(8,128)(2,1)}, f32[51...) custom-call(bf16[4,128,1024]{2,1,0:T(8,128)(2,1)} %x_in.1, ...), custom_call_target="tpu_custom_call" | custom-call | tf_op jit(solution)/shard_map/first/pallas_call | solution.py:697
  104.1 75.7 %backward.1 = (bf16[4,128,1024]{2,1,0:T(8,128)(2,1)}, bf16[4,128,1024]{2,1,0:T(8,128)(2,1)}, f32[8,3072]{1,0:T(8,128)}, f32[8,1024]{1,0:T(8,128)}, f32[8,4096]{1...) custom-call(f32[16,1024]{1,0:T(8,128)} %get-tuple-element.49.lse, f32[8,1024]{1,0:T(8,128)} %get-tuple-element.50.seg, ...), custom_call_target="tpu_custom_call" | custom-call | tf_op jit(solution)/shard_map/backward/pallas_call | solution.py:1064
  179.8 3.3 %finish.1 = (bf16[4,128,1024]{2,1,0:T(8,128)(2,1)}, bf16[4,128,1024]{2,1,0:T(8,128)(2,1)}, f32[8,3072]{1,0:T(8,128)}, f32[8,1024]{1,0:T(8,128)}, f32[8,4096]{1,0...) custom-call(bf16[4,128,1024]{2,1,0:T(8,128)(2,1)} %get-tuple-element, ...), custom_call_target="tpu_custom_call" | custom-call | tf_op jit(solution)/shard_map/finish/pallas_call | solution.py:1107

commit v4 on v3

--- a/solution.py
+++ b/solution.py
@@ -17,7 +17,8 @@
     (6, 8, ("x0", "z1", "z0"), ("x1", "y")),
 )
 OUT_ORDERS = (("y", "x", "z"), ("y", "z", "x"), ("y", "x", "z"), ("y", "z", "x"))
-QKV_ORDERS = (("x", "y", "z"), ("z", "x", "y"), ("y", "z", "x"))
+QKV_ORDERS = (("x", "z", "y"), ("z", "x", "y"), ("y", "z", "x"))
+LAG = {1: 2, 2: 3, 3: 4}
 BLOCK = 256
 GELU = 0.7978845608028654
 CUBIC = 0.044715
@@ -544,9 +545,9 @@
 
         for k in (3, 2, 1):
 
-            @pl.when(t >= k + 1)
+            @pl.when(t >= LAG[k])
             def _(k=k):
-                finish(k, t - k - 1)
+                finish(k, t - LAG[k])
 
         xh = lax.div(t, four)
         grad = dot_tn(act_s[...], cot[...]).astype(BF)
@@ -588,6 +589,11 @@
 
     lax.fori_loop(0, 8, tile, 0)
 
+    def rounds(n):
+        for k in (3, 2, 1):
+            if 0 <= n - LAG[k] < 8:
+                finish(k, n - LAG[k])
+
     dh_send, dh_got = qkv.at[0:512, 0:1024], qkv.at[512:1024, 0:1024]
     dn_send, dn_got = wq.at[0:512, 0:1024], wq.at[512:1024, 0:1024]
     dc_send = qkv.at[0:512, 1024:1536]
@@ -599,8 +605,7 @@
     dn_send[...] = down_acc[far, :].astype(BF)
     dn_copy = remote(dn_send, dn_got, es.at[1], er.at[1], mate)
     dn_copy.start()
-    for k in (3, 2, 1):
-        finish(k, 7 - k)
+    rounds(8)
 
     transpose_features(ctxp, ctxt, slice(0, 512))
     dh_copy.wait()
@@ -641,8 +646,7 @@
     dc_send[...] = dot_nt(dat[...], wo[far, :]).astype(BF)
     dc_copy = remote(dc_send, dctx.at[own], es.at[2], er.at[2], mate)
     dc_copy.start()
-    for k in (3, 2, 1):
-        finish(k, 8 - k)
+    rounds(9)
 
     def out_grad(cols, dst, lead):
         for b in range(4):
@@ -655,13 +659,13 @@
     wo_copy = remote(wo_send, wo_got, es.at[3], er.at[3], mate)
     wo_copy.start()
     dctx[own, :] = dot_nt(dat[...], wo[own, :]).astype(BF)
-    for k in (3, 2):
-        finish(k, 9 - k)
+    rounds(10)
     out_grad(own, bout, lambda j: (j,))
     dc_copy.wait_send()
     remote(dc_send, dctx.at[far], es.at[2], er.at[2], mate).wait_recv()
     saves(6, dctx, dctx_o).start()
-    finish(3, 7)
+    for n in range(11, 8 + LAG[3]):
+        rounds(n)
     saves(7, upleft, upleft_o).start()
     saves(8, downleft, downleft_o).start()
     wo_copy.wait()
@@ -724,11 +728,11 @@
 LEFT = (0, 1, 2, 3, 4)
 OUT = (5, 6, 7, 8)
 EVENTS = {
-    (0, 3): (("left", 1), ("early", 0)),
-    (1, 3): (("left", 2), ("early", 1)),
+    (1, 0): (("left", 1), ("early", 0)),
+    (2, 0): (("left", 2), ("early", 1)),
     (2, 1): (("out", 1),),
-    (2, 3): (("early", 2),),
-    (3, 1): (("out", 2),),
+    (3, 0): (("early", 2),),
+    (3, 2): (("out", 2),),
 }
 
 
@@ -797,7 +801,7 @@
             out_last()
 
     def vector_copy(ref, got, sends, recvs, n, s):
-        return remote(ref.at[n], got.at[n, s - 1], sends.at[n, s - 1], recvs.at[n, s - 1], place.ring("yxz"[n], s))
+        return remote(ref.at[n], got.at[n, s - 1], sends.at[n, s - 1], recvs.at[n, s - 1], place.ring("zxy"[n], s))
 
     def vector_start(ref, got, sends, recvs, n):
         for s in (1, 2, 3):
@@ -1012,13 +1016,13 @@
             dres[block, :]
             + rstd * (e - jnp.mean(e, axis=-1, keepdims=True) - xhat * jnp.mean(e * xhat, axis=-1, keepdims=True))
         ).astype(BF)
-        exchange_start(place, g_src, g_dst, g_dst, gs, gr, (2 * n, 2 * n + 1))
         if n == 0:
             vector_finish(late, late_got, vs, vr, 0)
-    tail(2)
-    main_finish(3, OUT)
+            tail(2)
+        exchange_start(place, g_src, g_dst, g_dst, gs, gr, (2 * n, 2 * n + 1))
     vector_finish(late, late_got, vs, vr, 1)
     tail(3)
+    main_finish(3, OUT)
     vector_finish(late, late_got, vs, vr, 2)
     late_copy.start()
     tail(4)

time: 184 us -> 180 us (0.978)
  Pallas kernels: 182 us -> 179 us
    pallas_call x1, Pallas kernels: 75.7 us -> 72.1 us  [run_backward(): pl.pallas_call(backward_kernel, out_shape=outs, in_specs=[vmem()] * 4 + [...]
where the time goes in v4:
time: 180 us
  Pallas kernels  179 us (99%)
    pallas_call x1, Pallas kernels, run_first(): pl.pallas_call(first_kernel, out_shape=outs, in_specs=[anywhere(), anywhe...  103 us
    pallas_call x1, Pallas kernels, run_backward(): pl.pallas_call(backward_kernel, out_shape=outs, in_specs=[vmem()] * 4 + [...  72.1 us

profile of v4, /device:TPU:1, one launch (start us, length us, event | category | flops | bytes accessed | tf_op | source)
XLA Modules:
  0.0 179.7 jit_solution(7712592262738774547)
XLA Ops:
  0.7 103.5 %first.1 = (bf16[1024,1024]{1,0:T(8,128)(2,1)}, bf16[1024,1536]{1,0:T(8,128)(2,1)}, bf16[512,1024]{1,0:T(8,128)(2,1)}, bf16[1024,512]{1,0:T(8,128)(2,1)}, f32[51...) custom-call(bf16[4,128,1024]{2,1,0:T(8,128)(2,1)} %x_in.1, ...), custom_call_target="tpu_custom_call" | custom-call | tf_op jit(solution)/shard_map/first/pallas_call | solution.py:701
  104.1 72.1 %backward.1 = (bf16[4,128,1024]{2,1,0:T(8,128)(2,1)}, bf16[4,128,1024]{2,1,0:T(8,128)(2,1)}, f32[8,3072]{1,0:T(8,128)}, f32[8,1024]{1,0:T(8,128)}, f32[8,4096]{1...) custom-call(f32[16,1024]{1,0:T(8,128)} %get-tuple-element.49.lse, f32[8,1024]{1,0:T(8,128)} %get-tuple-element.50.seg, ...), custom_call_target="tpu_custom_call" | custom-call | tf_op jit(solution)/shard_map/backward/pallas_call | solution.py:1068
  176.2 3.3 %finish.1 = (bf16[4,128,1024]{2,1,0:T(8,128)(2,1)}, bf16[4,128,1024]{2,1,0:T(8,128)(2,1)}, f32[8,3072]{1,0:T(8,128)}, f32[8,1024]{1,0:T(8,128)}, f32[8,4096]{1,0...) custom-call(bf16[4,128,1024]{2,1,0:T(8,128)(2,1)} %get-tuple-element, ...), custom_call_target="tpu_custom_call" | custom-call | tf_op jit(solution)/shard_map/finish/pallas_call | solution.py:1111

commit v5 on v4

--- a/solution.py
+++ b/solution.py
@@ -728,11 +728,11 @@
 LEFT = (0, 1, 2, 3, 4)
 OUT = (5, 6, 7, 8)
 EVENTS = {
-    (1, 0): (("left", 1), ("early", 0)),
-    (2, 0): (("left", 2), ("early", 1)),
-    (2, 1): (("out", 1),),
-    (3, 0): (("early", 2),),
-    (3, 2): (("out", 2),),
+    (1, 1): (("left", 1), ("early", 0)),
+    (2, 1): (("left", 2), ("early", 1)),
+    (2, 2): (("out", 1),),
+    (3, 1): (("early", 2),),
+    (3, 3): (("out", 2),),
 }
 
 

time: 180 us -> 179 us (level)
  no operation moved by 1% of the time
where the time goes in v5:
time: 179 us
  Pallas kernels  178 us (99%)
    pallas_call x1, Pallas kernels, run_first(): pl.pallas_call(first_kernel, out_shape=outs, in_specs=[anywhere(), anywhe...  103 us
    pallas_call x1, Pallas kernels, run_backward(): pl.pallas_call(backward_kernel, out_shape=outs, in_specs=[vmem()] * 4 + [...  71.1 us

profile of v5, /device:TPU:1, one launch (start us, length us, event | category | flops | bytes accessed | tf_op | source)
XLA Modules:
  0.0 178.6 jit_solution(1791789114977588870)
XLA Ops:
  0.7 103.5 %first.1 = (bf16[1024,1024]{1,0:T(8,128)(2,1)}, bf16[1024,1536]{1,0:T(8,128)(2,1)}, bf16[512,1024]{1,0:T(8,128)(2,1)}, bf16[1024,512]{1,0:T(8,128)(2,1)}, f32[51...) custom-call(bf16[4,128,1024]{2,1,0:T(8,128)(2,1)} %x_in.1, ...), custom_call_target="tpu_custom_call" | custom-call | tf_op jit(solution)/shard_map/first/pallas_call | solution.py:701
  104.1 71.1 %backward.1 = (bf16[4,128,1024]{2,1,0:T(8,128)(2,1)}, bf16[4,128,1024]{2,1,0:T(8,128)(2,1)}, f32[8,3072]{1,0:T(8,128)}, f32[8,1024]{1,0:T(8,128)}, f32[8,4096]{1...) custom-call(f32[16,1024]{1,0:T(8,128)} %get-tuple-element.49.lse, f32[8,1024]{1,0:T(8,128)} %get-tuple-element.50.seg, ...), custom_call_target="tpu_custom_call" | custom-call | tf_op jit(solution)/shard_map/backward/pallas_call | solution.py:1068
  175.2 3.3 %finish.1 = (bf16[4,128,1024]{2,1,0:T(8,128)(2,1)}, bf16[4,128,1024]{2,1,0:T(8,128)(2,1)}, f32[8,3072]{1,0:T(8,128)}, f32[8,1024]{1,0:T(8,128)}, f32[8,4096]{1,0...) custom-call(bf16[4,128,1024]{2,1,0:T(8,128)(2,1)} %get-tuple-element, ...), custom_call_target="tpu_custom_call" | custom-call | tf_op jit(solution)/shard_map/finish/pallas_call | solution.py:1111
